TPU v7x, 512 devices: a whole 4x8x8 slice. The times are simulated.
512 devices in a mesh: cuts: 8 (over x, core), tile: 64 (over y, z).
Axes of the slice: x: 4, y: 8, z: 8, core: 2. Of those that a mesh axis runs over, the one named last changes fastest.
Arguments:
- trans_real: float32 [8, 16384, 256], P('cuts', 'tile'), may hold values from 0.6 to 1.4
- trans_imag: float32 [8, 16384, 256], P('cuts', 'tile'), may hold values from -1.5 to 1.5
- probe_real: bfloat16 [128, 128], replicated, may hold values from -6 to 6
- probe_imag: bfloat16 [128, 128], replicated, may hold values from -6 to 6
- offsets: int32 [2, 2048], P(None, 'tile'), may hold values from 0 to 128
- pattern_index: int32 [2048], P('tile'), may hold values from 0 to 2047, as said below
- measured: bfloat16 [2048, 128, 128], P('tile'), may hold values from 0.19921875 to 3
Outputs:
- object_grad: float32 [2, 8, 16384, 256], P(None, 'cuts', 'tile')
Inputs may be any that keep to these rules, and one draw needn't show every extreme that they name: `pattern_index`: each row of measured is named by exactly one position; row r is stored with tile r // 32. Of the positions of one tile at most 1 have patterns stored with any one tile, and every tile has exactly 1 with some tile.
All inputs are finite; a program needn't handle non-finite values.
Results may differ from a plain program's by a relative error of at most 0.015.
The roundings to bfloat16 on the way count: a program that leaves them out, or rounds other values in their place, can miss the bound.
Values may be sent and summed in bfloat16 or wider, within the bound.
No kernel may reach another device: no remote copies, remote signals or barrier semaphores. Data moves between devices by JAX's collectives and lax.ppermute only.
A program may use at most 64 MiB of HBM per device.

v0:
```python
import math

import jax
import jax.numpy as jnp
from jax import lax
from jax.sharding import PartitionSpec as P

MICRO = 8


fresnel_strength = 9.0
softening = 0.01


def sent_together(arrays, axis, dim, along):
    ends, at = ([], 0)
    for a in arrays[:-1]:
        at += a.shape[along]
        ends.append(at)
    both = jnp.concatenate(arrays, axis=along)
    return tuple(
        jnp.split(lax.psum_scatter(both, axis, scatter_dimension=dim, tiled=True), ends, axis=along)
    )


def tables(extent):
    indices = jnp.arange(extent, dtype=jnp.int32)
    products = indices[:, None] * indices[None, :] % extent
    angles = products.astype(jnp.float32) * (2.0 * math.pi / extent)
    cosine = jnp.cos(angles)
    sines = jnp.sin(angles)
    frequency = (
        jnp.where(indices < (extent + 1) // 2, indices, indices - extent).astype(jnp.float32)
        / extent
    )
    phases = -fresnel_strength * frequency * frequency
    kernel_real = jnp.cos(phases)
    kernel_imag = jnp.sin(phases)
    scaled_real = cosine * kernel_real[None, :] - sines * kernel_imag[None, :]
    scaled_imag = cosine * kernel_imag[None, :] + sines * kernel_real[None, :]
    highest = lax.Precision.HIGHEST
    prop_real = (
        jnp.dot(scaled_real, cosine, precision=highest)
        + jnp.dot(scaled_imag, sines, precision=highest)
    ) / extent
    prop_imag = (
        jnp.dot(scaled_imag, cosine, precision=highest)
        - jnp.dot(scaled_real, sines, precision=highest)
    ) / extent
    norming = 1.0 / math.sqrt(extent)
    return (
        prop_real.astype(jnp.bfloat16),
        prop_imag.astype(jnp.bfloat16),
        (cosine * norming).astype(jnp.bfloat16),
        (-sines * norming).astype(jnp.bfloat16),
    )


def left_product(matrix, field):
    return jnp.einsum("ab,nbc->nac", matrix, field, preferred_element_type=jnp.float32)


def right_product(field, matrix):
    return jnp.einsum("nab,bc->nac", field, matrix, preferred_element_type=jnp.float32)


def apply_both(mat_real, mat_imag, field_real, field_imag):
    mid_real = (left_product(mat_real, field_real) - left_product(mat_imag, field_imag)).astype(
        jnp.bfloat16
    )
    mid_imag = (left_product(mat_real, field_imag) + left_product(mat_imag, field_real)).astype(
        jnp.bfloat16
    )
    end_real = right_product(mid_real, mat_real) - right_product(mid_imag, mat_imag)
    end_imag = right_product(mid_real, mat_imag) + right_product(mid_imag, mat_real)
    return (end_real, end_imag)


def windows(patch_grid, offset_sel, extent):

    def cut_one(row_at, col_at):
        return lax.dynamic_slice(patch_grid, (row_at, col_at), (extent, extent))

    return jax.vmap(cut_one)(offset_sel[0], offset_sel[1])


def accumulate(patch_grid, contrib, offset_sel, extent):

    def add_one(item, acc):
        row_at = offset_sel[0, item]
        col_at = offset_sel[1, item]
        current = lax.dynamic_slice(acc, (row_at, col_at), (extent, extent))
        return lax.dynamic_update_slice(acc, current + contrib[item], (row_at, col_at))

    return lax.fori_loop(0, contrib.shape[0], add_one, patch_grid)


def forward_slice(win_real, win_imag, wave_real, wave_imag, prop_real, prop_imag):
    field_real = (
        win_real * wave_real.astype(jnp.float32) - win_imag * wave_imag.astype(jnp.float32)
    ).astype(jnp.bfloat16)
    field_imag = (
        win_real * wave_imag.astype(jnp.float32) + win_imag * wave_real.astype(jnp.float32)
    ).astype(jnp.bfloat16)
    out_real, out_imag = apply_both(prop_real, prop_imag, field_real, field_imag)
    return jnp.stack([out_real.astype(jnp.bfloat16), out_imag.astype(jnp.bfloat16)])


def modulus(exit_real, exit_imag, amplitude, four_real, four_imag):
    far_real, far_imag = apply_both(four_real, four_imag, exit_real, exit_imag)
    amp = jnp.sqrt(far_real * far_real + far_imag * far_imag + softening)
    ratio = (amp - amplitude.astype(jnp.float32)) / amp
    resid_real = (ratio * far_real).astype(jnp.bfloat16)
    resid_imag = (ratio * far_imag).astype(jnp.bfloat16)
    back_real, back_imag = apply_both(four_real, -four_imag, resid_real, resid_imag)
    return (back_real.astype(jnp.bfloat16), back_imag.astype(jnp.bfloat16))


def backward_slice(
    win_real, win_imag, grad_real, grad_imag, wave_real, wave_imag, prop_real, prop_imag
):
    back_real, back_imag = apply_both(prop_real, -prop_imag, grad_real, grad_imag)
    psi_real = wave_real.astype(jnp.float32)
    psi_imag = wave_imag.astype(jnp.float32)
    contrib_real = back_real * psi_real + back_imag * psi_imag
    contrib_imag = back_imag * psi_real - back_real * psi_imag
    out_real = (back_real * win_real + back_imag * win_imag).astype(jnp.bfloat16)
    out_imag = (back_imag * win_real - back_real * win_imag).astype(jnp.bfloat16)
    return (contrib_real, contrib_imag, jnp.stack([out_real, out_imag]))


def fetch_patterns(pattern_index, measured, tile_count, capacity):
    positions = pattern_index.shape[0]
    owners = pattern_index // positions
    slots = pattern_index % positions
    ordinal = jnp.arange(positions, dtype=jnp.int32)
    shared = (owners[:, None] == owners[None, :]) & (ordinal[:, None] < ordinal[None, :])
    ranks = jnp.sum(shared.astype(jnp.int32), axis=0)
    target = owners * capacity + ranks
    request = jnp.zeros((tile_count * capacity,), jnp.int32).at[target].set(slots)
    requested = lax.all_to_all(request, "tile", split_axis=0, concat_axis=0, tiled=True)
    rows_out = jnp.take(measured, requested, axis=0)
    answered = lax.all_to_all(rows_out, "tile", split_axis=0, concat_axis=0, tiled=True)
    return jnp.take(answered, target, axis=0)


def local(trans_real, trans_imag, probe_real, probe_imag, offsets, pattern_index, measured):
    extent = probe_real.shape[-1]
    positions = pattern_index.shape[0]
    tile_count = lax.axis_size("tile")
    sections = lax.axis_size("cuts")
    section_no = lax.axis_index("cuts")
    capacity = (positions + tile_count - 1) // tile_count
    micro_count = MICRO
    per_batch = positions // micro_count
    prop_real, prop_imag, four_real, four_imag = tables(extent)
    amplitude = fetch_patterns(pattern_index, measured, tile_count, capacity)
    whole_real, whole_imag = (
        lax.all_gather(trans_real, "cuts", axis=0, tiled=True),
        lax.all_gather(trans_imag, "cuts", axis=0, tiled=True),
    )
    my_share = micro_count // sections
    mine_count = my_share * per_batch
    offset_mine = lax.dynamic_index_in_dim(
        offsets.reshape(2, my_share, sections, per_batch), section_no, 2, keepdims=False
    ).reshape(2, mine_count)
    amp_mine = lax.dynamic_index_in_dim(
        amplitude.reshape(my_share, sections, per_batch, extent, extent),
        section_no,
        1,
        keepdims=False,
    ).reshape(mine_count, extent, extent)
    probe_wave = jnp.stack(
        [
            jnp.broadcast_to(probe_real, (mine_count, extent, extent)),
            jnp.broadcast_to(probe_imag, (mine_count, extent, extent)),
        ]
    )

    def descend(wave_in, slab):
        slab_real, slab_imag = slab
        win_real = windows(slab_real, offset_mine, extent)
        win_imag = windows(slab_imag, offset_mine, extent)
        out_wave = forward_slice(win_real, win_imag, wave_in[0], wave_in[1], prop_real, prop_imag)
        return (out_wave, wave_in)

    exit_wave, stored = lax.scan(descend, probe_wave, (whole_real, whole_imag))
    seed_real, seed_imag = modulus(exit_wave[0], exit_wave[1], amp_mine, four_real, four_imag)
    grid_zero = jnp.zeros(whole_real.shape[1:], jnp.float32)

    def ascend(wave_in, slab):
        slab_real, slab_imag, psi_wave = slab
        win_real = windows(slab_real, offset_mine, extent)
        win_imag = windows(slab_imag, offset_mine, extent)
        contrib_real, contrib_imag, out_wave = backward_slice(
            win_real,
            win_imag,
            wave_in[0],
            wave_in[1],
            psi_wave[0],
            psi_wave[1],
            prop_real,
            prop_imag,
        )
        grad_real = accumulate(grid_zero, contrib_real, offset_mine, extent)
        grad_imag = accumulate(grid_zero, contrib_imag, offset_mine, extent)
        return (out_wave, (grad_real, grad_imag))

    _, slab_grads = lax.scan(
        ascend, jnp.stack([seed_real, seed_imag]), (whole_real, whole_imag, stored), reverse=True
    )
    part_real, part_imag = sent_together((slab_grads[0], slab_grads[1]), "cuts", 0, 1)
    return jnp.stack([part_real, part_imag])


def solution(mesh):
    return jax.shard_map(
        local,
        mesh=mesh,
        in_specs=(
            P("cuts", "tile", None),
            P("cuts", "tile", None),
            P(),
            P(),
            P(None, "tile"),
            P("tile"),
            P("tile", None, None),
        ),
        out_specs=P(None, "cuts", "tile", None),
        check_vma=False,
    )
```

profile of v0, /device:TPU:1, one launch (start us, length us, event | category | flops | bytes accessed | tf_op | source)
XLA Modules:
  0.0 894.7 jit_solution(13409643915595887316)
XLA Ops:
  10.2 17.1 %all-to-all-start = ((s32[64,1,1]{2,1,0:T(1,128)}), s32[64,1,1]{2,1,0:T(1,128)S(1)}, u32[]{:S(2)}, u32[]{:S(2)}) async-start(s32[64,1,1]{2,1,0:T(1,128)} %copy.142), calls=%async_computation | async-start | bytes 65536 | tf_op jit(solution)/shard_map/all_to_all | solution.py:141
  48.3 30.9 %all-gather.5.cloned.1.call-done = f32[8,256,256]{2,1,0:T(8,128)} async-done(((f32[1,256,256]{2,1,0:T(8,128)}), f32[8,256,256]{2,1,0:T(8,128)}) %all-gather.5.cloned.1.call-update) | async-done | bytes 2097168 | tf_op jit(solution)/shard_map/all_gather | solution.py:160
  79.2 159.8 %while.92 = (s32[]{:T(128)}, bf16[2,4,128,128]{3,2,1,0:T(8,128)(2,1)S(1)}, bf16[8,2,4,128,128]{4,3,2,1,0:T(8,128)(2,1)}, f32[8,256,256]{2,1,0:T(8,128)}, s32[2,4...) while((s32[]{:T(128)}, ...), condition=%wide.region_1.2_spmd, body=%wide.region_0.1_spmd.sunk | while | flops 135528480 | bytes 7864927 | solution.py:187
  80.4 8.3 while.98
  88.6 7.9 while.99
  100.3 8.3 while.98
  120.3 8.3 while.98
  140.3 8.3 while.98
  160.3 8.3 while.98
  168.6 7.9 while.99
  180.3 8.3 while.98
  200.2 8.3 while.98
  208.5 7.9 while.99
  220.2 8.3 while.98
  251.8 585.5 %while.97 = (s32[]{:T(128)}, bf16[2,4,128,128]{3,2,1,0:T(8,128)(2,1)S(1)}, f32[8,256,256]{2,1,0:T(8,128)}, f32[8,256,256]{2,1,0:T(8,128)}, bf16[128,128]{1,0:T(8...) while((s32[]{:T(128)}, ...), condition=%wide.region_9.10_spmd, body=%wide.region_4.9_spmd.sunk | while | flops 135823392 | bytes 10880205 | solution.py:209
  255.4 8.2 while.100
  263.7 8.4 while.101
  273.4 25.8 %while.102 = (s32[]{:T(128)}, f32[256,256]{1,0:T(8,128)S(1)}, s32[2,4]{1,0:T(2,128)S(1)}, f32[4,128,128]{2,1,0:T(8,128)S(1)}, s32[]{:T(128)}, /*index=5*/s32[]{:T(128)}, s32[]{:T(128)}) while((s32[]{:T(128)}, f32[256,256]{1,0:T(8,128)S(1)}, s32[2,4]{1,0:T(2,128)S(1)}, f32[4,128,128]{2,1,0:T(8,128)S(1)}, s32[]{:T(128)}, /*index=5*/s32[]{:T(128)}, ...), condition=%wide.region_8.8_spmd, body=%wide.region_7.7_spmd.sunk | while | flops 16392 | bytes 327869 | solution.py:95
  299.3 24.9 %while.103 = (s32[]{:T(128)}, f32[256,256]{1,0:T(8,128)S(1)}, s32[2,4]{1,0:T(2,128)S(1)}, f32[4,128,128]{2,1,0:T(8,128)S(1)}, s32[]{:T(128)}, /*index=5*/s32[]{:T(128)}, s32[]{:T(128)}) while((s32[]{:T(128)}, f32[256,256]{1,0:T(8,128)S(1)}, s32[2,4]{1,0:T(2,128)S(1)}, f32[4,128,128]{2,1,0:T(8,128)S(1)}, s32[]{:T(128)}, /*index=5*/s32[]{:T(128)}, ...), condition=%wide.region_6.6_spmd, body=%wide.region_5.5_spmd.sunk | while | flops 16392 | bytes 327869 | solution.py:95
  328.6 8.2 while.100
  336.9 8.4 while.101
  346.6 25.8 %while.102 = (s32[]{:T(128)}, f32[256,256]{1,0:T(8,128)S(1)}, s32[2,4]{1,0:T(2,128)S(1)}, f32[4,128,128]{2,1,0:T(8,128)S(1)}, s32[]{:T(128)}, /*index=5*/s32[]{:T(128)}, s32[]{:T(128)}) while((s32[]{:T(128)}, f32[256,256]{1,0:T(8,128)S(1)}, s32[2,4]{1,0:T(2,128)S(1)}, f32[4,128,128]{2,1,0:T(8,128)S(1)}, s32[]{:T(128)}, /*index=5*/s32[]{:T(128)}, ...), condition=%wide.region_8.8_spmd, body=%wide.region_7.7_spmd.sunk | while | flops 16392 | bytes 327869 | solution.py:95
  372.5 24.9 %while.103 = (s32[]{:T(128)}, f32[256,256]{1,0:T(8,128)S(1)}, s32[2,4]{1,0:T(2,128)S(1)}, f32[4,128,128]{2,1,0:T(8,128)S(1)}, s32[]{:T(128)}, /*index=5*/s32[]{:T(128)}, s32[]{:T(128)}) while((s32[]{:T(128)}, f32[256,256]{1,0:T(8,128)S(1)}, s32[2,4]{1,0:T(2,128)S(1)}, f32[4,128,128]{2,1,0:T(8,128)S(1)}, s32[]{:T(128)}, /*index=5*/s32[]{:T(128)}, ...), condition=%wide.region_6.6_spmd, body=%wide.region_5.5_spmd.sunk | while | flops 16392 | bytes 327869 | solution.py:95
  401.8 8.2 while.100
  410.1 8.4 while.101
  419.8 25.8 %while.102 = (s32[]{:T(128)}, f32[256,256]{1,0:T(8,128)S(1)}, s32[2,4]{1,0:T(2,128)S(1)}, f32[4,128,128]{2,1,0:T(8,128)S(1)}, s32[]{:T(128)}, /*index=5*/s32[]{:T(128)}, s32[]{:T(128)}) while((s32[]{:T(128)}, f32[256,256]{1,0:T(8,128)S(1)}, s32[2,4]{1,0:T(2,128)S(1)}, f32[4,128,128]{2,1,0:T(8,128)S(1)}, s32[]{:T(128)}, /*index=5*/s32[]{:T(128)}, ...), condition=%wide.region_8.8_spmd, body=%wide.region_7.7_spmd.sunk | while | flops 16392 | bytes 327869 | solution.py:95
  445.7 24.9 %while.103 = (s32[]{:T(128)}, f32[256,256]{1,0:T(8,128)S(1)}, s32[2,4]{1,0:T(2,128)S(1)}, f32[4,128,128]{2,1,0:T(8,128)S(1)}, s32[]{:T(128)}, /*index=5*/s32[]{:T(128)}, s32[]{:T(128)}) while((s32[]{:T(128)}, f32[256,256]{1,0:T(8,128)S(1)}, s32[2,4]{1,0:T(2,128)S(1)}, f32[4,128,128]{2,1,0:T(8,128)S(1)}, s32[]{:T(128)}, /*index=5*/s32[]{:T(128)}, ...), condition=%wide.region_6.6_spmd, body=%wide.region_5.5_spmd.sunk | while | flops 16392 | bytes 327869 | solution.py:95
  475.0 8.2 while.100
  483.2 8.4 while.101
  493.0 25.8 %while.102 = (s32[]{:T(128)}, f32[256,256]{1,0:T(8,128)S(1)}, s32[2,4]{1,0:T(2,128)S(1)}, f32[4,128,128]{2,1,0:T(8,128)S(1)}, s32[]{:T(128)}, /*index=5*/s32[]{:T(128)}, s32[]{:T(128)}) while((s32[]{:T(128)}, f32[256,256]{1,0:T(8,128)S(1)}, s32[2,4]{1,0:T(2,128)S(1)}, f32[4,128,128]{2,1,0:T(8,128)S(1)}, s32[]{:T(128)}, /*index=5*/s32[]{:T(128)}, ...), condition=%wide.region_8.8_spmd, body=%wide.region_7.7_spmd.sunk | while | flops 16392 | bytes 327869 | solution.py:95
  518.8 24.9 %while.103 = (s32[]{:T(128)}, f32[256,256]{1,0:T(8,128)S(1)}, s32[2,4]{1,0:T(2,128)S(1)}, f32[4,128,128]{2,1,0:T(8,128)S(1)}, s32[]{:T(128)}, /*index=5*/s32[]{:T(128)}, s32[]{:T(128)}) while((s32[]{:T(128)}, f32[256,256]{1,0:T(8,128)S(1)}, s32[2,4]{1,0:T(2,128)S(1)}, f32[4,128,128]{2,1,0:T(8,128)S(1)}, s32[]{:T(128)}, /*index=5*/s32[]{:T(128)}, ...), condition=%wide.region_6.6_spmd, body=%wide.region_5.5_spmd.sunk | while | flops 16392 | bytes 327869 | solution.py:95
  548.2 8.2 while.100
  556.4 8.4 while.101
  566.2 25.8 %while.102 = (s32[]{:T(128)}, f32[256,256]{1,0:T(8,128)S(1)}, s32[2,4]{1,0:T(2,128)S(1)}, f32[4,128,128]{2,1,0:T(8,128)S(1)}, s32[]{:T(128)}, /*index=5*/s32[]{:T(128)}, s32[]{:T(128)}) while((s32[]{:T(128)}, f32[256,256]{1,0:T(8,128)S(1)}, s32[2,4]{1,0:T(2,128)S(1)}, f32[4,128,128]{2,1,0:T(8,128)S(1)}, s32[]{:T(128)}, /*index=5*/s32[]{:T(128)}, ...), condition=%wide.region_8.8_spmd, body=%wide.region_7.7_spmd.sunk | while | flops 16392 | bytes 327869 | solution.py:95
  592.0 24.9 %while.103 = (s32[]{:T(128)}, f32[256,256]{1,0:T(8,128)S(1)}, s32[2,4]{1,0:T(2,128)S(1)}, f32[4,128,128]{2,1,0:T(8,128)S(1)}, s32[]{:T(128)}, /*index=5*/s32[]{:T(128)}, s32[]{:T(128)}) while((s32[]{:T(128)}, f32[256,256]{1,0:T(8,128)S(1)}, s32[2,4]{1,0:T(2,128)S(1)}, f32[4,128,128]{2,1,0:T(8,128)S(1)}, s32[]{:T(128)}, /*index=5*/s32[]{:T(128)}, ...), condition=%wide.region_6.6_spmd, body=%wide.region_5.5_spmd.sunk | while | flops 16392 | bytes 327869 | solution.py:95
  621.3 8.2 while.100
  629.6 8.4 while.101
  639.3 25.8 %while.102 = (s32[]{:T(128)}, f32[256,256]{1,0:T(8,128)S(1)}, s32[2,4]{1,0:T(2,128)S(1)}, f32[4,128,128]{2,1,0:T(8,128)S(1)}, s32[]{:T(128)}, /*index=5*/s32[]{:T(128)}, s32[]{:T(128)}) while((s32[]{:T(128)}, f32[256,256]{1,0:T(8,128)S(1)}, s32[2,4]{1,0:T(2,128)S(1)}, f32[4,128,128]{2,1,0:T(8,128)S(1)}, s32[]{:T(128)}, /*index=5*/s32[]{:T(128)}, ...), condition=%wide.region_8.8_spmd, body=%wide.region_7.7_spmd.sunk | while | flops 16392 | bytes 327869 | solution.py:95
  665.2 24.9 %while.103 = (s32[]{:T(128)}, f32[256,256]{1,0:T(8,128)S(1)}, s32[2,4]{1,0:T(2,128)S(1)}, f32[4,128,128]{2,1,0:T(8,128)S(1)}, s32[]{:T(128)}, /*index=5*/s32[]{:T(128)}, s32[]{:T(128)}) while((s32[]{:T(128)}, f32[256,256]{1,0:T(8,128)S(1)}, s32[2,4]{1,0:T(2,128)S(1)}, f32[4,128,128]{2,1,0:T(8,128)S(1)}, s32[]{:T(128)}, /*index=5*/s32[]{:T(128)}, ...), condition=%wide.region_6.6_spmd, body=%wide.region_5.5_spmd.sunk | while | flops 16392 | bytes 327869 | solution.py:95
  694.5 8.2 while.100
  702.8 8.4 while.101
  712.5 25.8 %while.102 = (s32[]{:T(128)}, f32[256,256]{1,0:T(8,128)S(1)}, s32[2,4]{1,0:T(2,128)S(1)}, f32[4,128,128]{2,1,0:T(8,128)S(1)}, s32[]{:T(128)}, /*index=5*/s32[]{:T(128)}, s32[]{:T(128)}) while((s32[]{:T(128)}, f32[256,256]{1,0:T(8,128)S(1)}, s32[2,4]{1,0:T(2,128)S(1)}, f32[4,128,128]{2,1,0:T(8,128)S(1)}, s32[]{:T(128)}, /*index=5*/s32[]{:T(128)}, ...), condition=%wide.region_8.8_spmd, body=%wide.region_7.7_spmd.sunk | while | flops 16392 | bytes 327869 | solution.py:95
  738.4 24.9 %while.103 = (s32[]{:T(128)}, f32[256,256]{1,0:T(8,128)S(1)}, s32[2,4]{1,0:T(2,128)S(1)}, f32[4,128,128]{2,1,0:T(8,128)S(1)}, s32[]{:T(128)}, /*index=5*/s32[]{:T(128)}, s32[]{:T(128)}) while((s32[]{:T(128)}, f32[256,256]{1,0:T(8,128)S(1)}, s32[2,4]{1,0:T(2,128)S(1)}, f32[4,128,128]{2,1,0:T(8,128)S(1)}, s32[]{:T(128)}, /*index=5*/s32[]{:T(128)}, ...), condition=%wide.region_6.6_spmd, body=%wide.region_5.5_spmd.sunk | while | flops 16392 | bytes 327869 | solution.py:95
  767.7 8.2 while.100
  776.0 8.4 while.101
  785.7 25.8 %while.102 = (s32[]{:T(128)}, f32[256,256]{1,0:T(8,128)S(1)}, s32[2,4]{1,0:T(2,128)S(1)}, f32[4,128,128]{2,1,0:T(8,128)S(1)}, s32[]{:T(128)}, /*index=5*/s32[]{:T(128)}, s32[]{:T(128)}) while((s32[]{:T(128)}, f32[256,256]{1,0:T(8,128)S(1)}, s32[2,4]{1,0:T(2,128)S(1)}, f32[4,128,128]{2,1,0:T(8,128)S(1)}, s32[]{:T(128)}, /*index=5*/s32[]{:T(128)}, ...), condition=%wide.region_8.8_spmd, body=%wide.region_7.7_spmd.sunk | while | flops 16392 | bytes 327869 | solution.py:95
  811.6 24.9 %while.103 = (s32[]{:T(128)}, f32[256,256]{1,0:T(8,128)S(1)}, s32[2,4]{1,0:T(2,128)S(1)}, f32[4,128,128]{2,1,0:T(8,128)S(1)}, s32[]{:T(128)}, /*index=5*/s32[]{:T(128)}, s32[]{:T(128)}) while((s32[]{:T(128)}, f32[256,256]{1,0:T(8,128)S(1)}, s32[2,4]{1,0:T(2,128)S(1)}, f32[4,128,128]{2,1,0:T(8,128)S(1)}, s32[]{:T(128)}, /*index=5*/s32[]{:T(128)}, ...), condition=%wide.region_6.6_spmd, body=%wide.region_5.5_spmd.sunk | while | flops 16392 | bytes 327869 | solution.py:95
  841.8 44.5 %reduce-scatter.2.cloned.1.call-done = f32[1,512,256]{2,1,0:T(8,128)} async-done(((f32[8,512,256]{2,1,0:T(8,128)}), f32[1,512,256]{2,1,0:T(8,128)}) %reduce-scatter.2.cloned.1.call-update) | async-done | bytes 524304 | tf_op jit(solution)/shard_map/reduce_scatter | solution.py:22
  (922 shorter events, 585.7 us)
Async XLA Ops:
  6.5 32.8 %copy-start = (bf16[32,128,128]{2,1,0:T(8,128)(2,1)S(1)}, bf16[32,128,128]{2,1,0:T(8,128)(2,1)}, u32[]{:S(2)}) copy-start(bf16[32,128,128]{2,1,0:T(8,128)(2,1)} %param.21) | copy-start | bytes 3145732
  6.5 41.8 %all-gather.3.cloned.1.call-start = ((), (), s32[]{:S(2)}) async-start(), calls=%async_computation.3 | async-start | bytes 2359296 | tf_op jit(solution)/shard_map/all_gather | solution.py:159
  7.3 72.0 %all-gather.5.cloned.1.call-start = ((), (), s32[]{:S(2)}) async-start(), calls=%async_computation.4 | async-start | bytes 2359296 | tf_op jit(solution)/shard_map/all_gather | solution.py:160
  10.2 27.9 %all-to-all-start = ((s32[64,1,1]{2,1,0:T(1,128)}), s32[64,1,1]{2,1,0:T(1,128)S(1)}, u32[]{:S(2)}, u32[]{:S(2)}) async-start(s32[64,1,1]{2,1,0:T(1,128)} %copy.142), calls=%async_computation | async-start | bytes 65536 | tf_op jit(solution)/shard_map/all_to_all | solution.py:141
  42.0 200.3 %all-to-all-start.1 = ((bf16[64,128,128]{2,1,0:T(8,128)(2,1)}), bf16[64,128,128]{2,1,0:T(8,128)(2,1)}, u32[]{:S(2)}, u32[]{:S(2)}) async-start(bf16[64,128,128]{2,1,0:T(8,128)(2,1)} %broadcast_select_fusion), calls=%async_computation.1 | async-start | bytes 4194304 | tf_op jit(solution)/shard_map/all_to_all | solution.py:143
  48.1 838.2 %reduce-scatter.2.cloned.1.call-start = ((), (), s32[]{:S(2)}) async-start(), calls=%async_computation.5 | async-start | bytes 4718592 | tf_op jit(solution)/shard_map/reduce_scatter | solution.py:22
Sparse Core Ops, SparseCore 0:
  9.5 36.4 all-gather.2
  48.1 31.0 all-gather.4
  841.9 44.3 reduce-scatter.1
where the time goes:
time: 902 us; the launch traced here: 895 us
  local copies, waits for them, and re-layouts  472 us (52%)
  loops' own time  243 us (27%)
  waiting for transfers between devices  83.2 us (9%)
  matrix products  43.8 us (5%)
  starting transfers between devices  23.5 us (3%)
  other arithmetic  16.7 us (2%)
  between operations  13.4 us (1%)
    gather x384, local copies, waits for them, and re-layouts  260 us
    another operation x16, loops' own time, accumulate(): return lax.fori_loop(0, contrib.shape[0], add_one, patch_grid)  238 us
    dynamic_update_slice x64, local copies, waits for them, and re-layouts, add_one(): lax.dynamic_update_slice(acc, current + contrib[item], (row_at, col_at))  123 us
    reduce_scatter x1, waiting for transfers between devices, sent_together(): lax.psum_scatter(both, axis, scatter_dimension=dim, tiled=True)  44.5 us
    dynamic_slice x64, local copies, waits for them, and re-layouts, add_one(): col_at = offset_sel[1, item]  38 us
    all_gather x1, waiting for transfers between devices, local(): lax.all_gather(trans_imag, 'cuts', axis=0, tiled=True)  30.9 us
    dot_general x72, matrix products, right_product(): jnp.einsum('nab,bc->nac', field, matrix, preferred_element_type=jnp.float32)  25.7 us
    squeeze x24, local copies, waits for them, and re-layouts, local(): exit_wave, stored = lax.scan(descend, probe_wave, (whole_real, whole_imag))  24.2 us
  transfers between devices with their start and end apart: 5, of which 3 were waited for; matrix products, arithmetic and copies ran while one was open for 19% of the time, Pallas kernels for 0%

commit v1 on v0

v1 whole, which is shorter than its diff:
```python
import math

import jax
import jax.numpy as jnp
import ml_dtypes
import numpy as np
from jax import lax
from jax.experimental import pallas as pl
from jax.experimental.pallas import tpu as pltpu
from jax.sharding import PartitionSpec as P

fresnel_strength = 9.0
softening = 0.01

CODE_TOP = 32766.0
REAL_MID = 1.0
REAL_HALF = 0.4
IMAG_HALF = 1.5


def tables(extent):
    indices = np.arange(extent)
    angles = (indices[:, None] * indices[None, :] % extent) * (2.0 * math.pi / extent)
    whole = np.cos(angles) + 1j * np.sin(angles)
    frequency = np.where(indices < (extent + 1) // 2, indices, indices - extent) / extent
    prop = (whole * np.exp(-1j * fresnel_strength * frequency**2)[None, :]) @ whole.conj() / extent
    four = whole.conj() / math.sqrt(extent)
    blocks = []
    for matrix in (prop, four):
        real = matrix.real.astype(np.float32).astype(ml_dtypes.bfloat16)
        imag = matrix.imag.astype(np.float32).astype(ml_dtypes.bfloat16)
        blocks.append(np.block([[real, -imag], [imag, real]]))
        blocks.append(np.block([[real, imag], [-imag, real]]))
    return np.stack(blocks).astype(ml_dtypes.bfloat16)


def encode(trans_real, trans_imag):
    real = jnp.round((trans_real - REAL_MID) * (CODE_TOP / REAL_HALF)).astype(jnp.int32)
    imag = jnp.round(trans_imag * (CODE_TOP / IMAG_HALF)).astype(jnp.int32)
    return (real << 16) | (imag & 0xFFFF)


def decode(code):
    real = (code >> 16).astype(jnp.float32) * (REAL_HALF / CODE_TOP) + REAL_MID
    imag = ((code << 16) >> 16).astype(jnp.float32) * (IMAG_HALF / CODE_TOP)
    return real, imag


def quarters(square):
    half = square.shape[0] // 2
    return (square[:half, :half], square[:half, half:], square[half:, :half], square[half:, half:])


def joined(a, b, c, d):
    return jnp.concatenate(
        [jnp.concatenate([a, b], axis=1), jnp.concatenate([c, d], axis=1)], axis=0
    )


def both_sides(left, right, field):
    real0, imag0, real1, imag1 = quarters(field)
    mid = jnp.dot(
        left, joined(real0, real1, imag0, imag1), preferred_element_type=jnp.float32
    ).astype(jnp.bfloat16)
    real0, real1, imag0, imag1 = quarters(mid)
    return jnp.dot(
        joined(real0, imag0, real1, imag1), right, preferred_element_type=jnp.float32
    )


def gradient_kernel(
    offset_ref, patch_ref, probe_ref, amp_ref, table_ref, out_ref, code_ref, wave_ref, grad_ref, sum_ref
):
    slices, side, _ = patch_ref.shape
    extent = probe_ref.shape[1]
    count = code_ref.shape[1]
    pairs = count // 2
    pieces, _, piece_rows, _ = amp_ref.shape

    tall = extent + 8

    def placed(position):
        row_at = offset_ref[0, position]
        start = jnp.minimum(row_at // 8, (side - tall) // 8) * 8
        return pl.multiple_of(start, 8), row_at - start

    def part(pair, item):
        return pair * 2 + item, slice(item * extent, (item + 1) * extent)

    for pair in range(pairs):
        for item in range(2):
            _, rows = part(pair, item)
            wave_ref[0, pair, rows, :extent] = probe_ref[0]
            wave_ref[0, pair, rows, extent:] = probe_ref[1]

    def descend(layer, carry):
        for pair in range(pairs):
            fields = []
            for item in range(2):
                position, rows = part(pair, item)
                row_at, down = placed(position)
                back = lax.rem(side - offset_ref[1, position], side)
                code = pltpu.roll(patch_ref[layer, pl.ds(row_at, tall), :], back, 1)[:, :extent]
                code = pltpu.roll(code, lax.rem(tall - down, tall), 0)[:extent]
                code_ref[layer, position] = code
                t_real, t_imag = decode(code)
                wave = wave_ref[layer, pair, rows, :].astype(jnp.float32)
                w_real, w_imag = wave[:, :extent], wave[:, extent:]
                fields.append(
                    jnp.concatenate(
                        [t_real * w_real - t_imag * w_imag, t_real * w_imag + t_imag * w_real], axis=1
                    ).astype(jnp.bfloat16)
                )
            ahead = both_sides(table_ref[0], table_ref[1], jnp.concatenate(fields, axis=0))
            wave_ref[layer + 1, pair] = ahead.astype(jnp.bfloat16)
        return carry

    lax.fori_loop(0, slices, descend, 0)

    for pair in range(pairs):
        far = both_sides(table_ref[2], table_ref[3], wave_ref[slices, pair])
        residue = []
        for item in range(2):
            position, rows = part(pair, item)
            f_real, f_imag = far[rows, :extent], far[rows, extent:]
            amplitude = jnp.concatenate(
                [amp_ref[piece, position] for piece in range(pieces)], axis=0
            ).astype(jnp.float32)
            amp = jnp.sqrt(f_real * f_real + f_imag * f_imag + softening)
            ratio = (amp - amplitude) / amp
            residue.append(
                jnp.concatenate([ratio * f_real, ratio * f_imag], axis=1).astype(jnp.bfloat16)
            )
        back = both_sides(table_ref[3], table_ref[2], jnp.concatenate(residue, axis=0))
        grad_ref[pair] = back.astype(jnp.bfloat16)

    def ascend(step, carry):
        layer = slices - 1 - step
        sum_ref[...] = jnp.zeros_like(sum_ref)
        for pair in range(pairs):
            back = both_sides(table_ref[1], table_ref[0], grad_ref[pair])
            for item in range(2):
                position, rows = part(pair, item)
                u_real, u_imag = back[rows, :extent], back[rows, extent:]
                t_real, t_imag = decode(code_ref[layer, position])
                grad_ref[pair, rows, :extent] = (u_real * t_real + u_imag * t_imag).astype(jnp.bfloat16)
                grad_ref[pair, rows, extent:] = (u_imag * t_real - u_real * t_imag).astype(jnp.bfloat16)
                wave = wave_ref[layer, pair, rows, :].astype(jnp.float32)
                w_real, w_imag = wave[:, :extent], wave[:, extent:]
                row_at, down = placed(position)
                col_at = offset_ref[1, position]
                for plane, contrib in enumerate(
                    (u_real * w_real + u_imag * w_imag, u_imag * w_real - u_real * w_imag)
                ):
                    high = jnp.concatenate(
                        [contrib, jnp.zeros((tall - extent, extent), jnp.float32)], axis=0
                    )
                    wide = jnp.concatenate(
                        [pltpu.roll(high, down, 0), jnp.zeros((tall, side - extent), jnp.float32)],
                        axis=1,
                    )
                    sum_ref[plane, pl.ds(row_at, tall), :] += pltpu.roll(wide, col_at, 1)
        out_ref[layer, :side] = sum_ref[0].astype(jnp.bfloat16)
        out_ref[layer, side:] = sum_ref[1].astype(jnp.bfloat16)
        return carry

    lax.fori_loop(0, slices, ascend, 0)


def patch_gradient(offset_mine, patches, probe, amp_pieces, table):
    slices, side, _ = patches.shape
    extent = probe.shape[-1]
    count = offset_mine.shape[1]
    vmem = pl.BlockSpec(memory_space=pltpu.VMEM)
    return pl.pallas_call(
        gradient_kernel,
        out_shape=jax.ShapeDtypeStruct((slices, 2 * side, side), jnp.bfloat16),
        in_specs=[pl.BlockSpec(memory_space=pltpu.SMEM), vmem, vmem, vmem, vmem],
        out_specs=vmem,
        scratch_shapes=[
            pltpu.VMEM((slices, count, extent, extent), jnp.int32),
            pltpu.VMEM((slices + 1, count // 2, 2 * extent, 2 * extent), jnp.bfloat16),
            pltpu.VMEM((count // 2, 2 * extent, 2 * extent), jnp.bfloat16),
            pltpu.VMEM((2, side, side), jnp.float32),
        ],
        name="patch_gradient",
        compiler_params=pltpu.CompilerParams(vmem_limit_bytes=40 << 20),
        cost_estimate=pl.CostEstimate(
            flops=2 * (slices + 1) * 2 * count * 8 * extent**3, bytes_accessed=6 << 20, transcendentals=0
        ),
    )(offset_mine, patches, probe, amp_pieces, table)


def fetch_patterns(pattern_index, measured, section_no, sections):
    positions = pattern_index.shape[0]
    tile_count = lax.axis_size("tile")
    extent = measured.shape[1]
    share = extent // sections
    owners = pattern_index // positions
    slots = pattern_index % positions
    named = owners[None, :] == jnp.arange(tile_count, dtype=jnp.int32)[:, None]
    request = jnp.sum(jnp.where(named, slots[None, :], 0), axis=1)
    requested = lax.all_to_all(request, "tile", split_axis=0, concat_axis=0, tiled=True)
    mine = lax.dynamic_slice_in_dim(measured, section_no * share, share, 1)
    answered = lax.all_to_all(
        jnp.take(mine, requested, axis=0), "tile", split_axis=0, concat_axis=0, tiled=True
    )
    return jnp.take(answered, owners, axis=0)


def local(trans_real, trans_imag, probe_real, probe_imag, offsets, pattern_index, measured):
    extent = probe_real.shape[-1]
    side = trans_real.shape[-1]
    positions = pattern_index.shape[0]
    sections = lax.axis_size("cuts")
    section_no = lax.axis_index("cuts")
    per_batch = positions // sections
    table = jnp.asarray(tables(extent))
    pieces = fetch_patterns(pattern_index, measured, section_no, sections)
    amp_pieces = lax.all_to_all(
        pieces.reshape(sections, per_batch, extent // sections, extent),
        "cuts",
        split_axis=0,
        concat_axis=0,
        tiled=True,
    )
    patches = lax.all_gather(encode(trans_real, trans_imag), "cuts", axis=0, tiled=True)
    offset_mine = lax.dynamic_slice_in_dim(offsets, section_no * per_batch, per_batch, 1)
    partial = patch_gradient(
        offset_mine, patches, jnp.stack([probe_real, probe_imag]), amp_pieces, table
    )
    parts = lax.all_to_all(partial, "cuts", split_axis=0, concat_axis=0, tiled=True)
    total = jnp.sum(parts.astype(jnp.float32), axis=0)
    return total.reshape(2, 1, side, side)


def solution(mesh):
    return jax.shard_map(
        local,
        mesh=mesh,
        in_specs=(
            P("cuts", "tile", None),
            P("cuts", "tile", None),
            P(),
            P(),
            P(None, "tile"),
            P("tile"),
            P("tile", None, None),
        ),
        out_specs=P(None, "cuts", "tile", None),
        check_vma=False,
    )
```

time: 902 us -> 126 us (0.14)
  local copies, waits for them, and re-layouts: 472 us -> 3.72 us
  loops' own time: 243 us -> 0 us
  waiting for transfers between devices: 83.2 us -> 28.4 us
  matrix products: 43.8 us -> 0 us
  blocking collectives: 0 us -> 29.5 us
  Pallas kernels: 0 us -> 13.5 us
  other arithmetic: 16.7 us -> 7.26 us
    gather x386 -> x2, local copies, waits for them, and re-layouts: 263 us -> 1.22 us  [the longest x1 0.63 us: fetch_patterns(): jnp.take(mine, requested, axis=0)]
    another operation x50 -> x0, loops' own time: 243 us -> none  [the longest x16 238 us: accumulate(): return lax.fori_loop(0, contrib.shape[0], add_one, patch_grid)]
    dynamic_update_slice x80 -> x0, local copies, waits for them, and re-layouts: 136 us -> none  [the longest x64 123 us: add_one(): lax.dynamic_update_slice(acc, current + contrib[item], (row_at, col_at))]
    reduce_scatter x1 -> x0, waiting for transfers between devices: 44.5 us -> none  [sent_together(): lax.psum_scatter(both, axis, scatter_dimension=dim, tiled=True)]
    dot_general x148 -> x0, matrix products: 43.8 us -> none  [the longest x72 25.7 us: right_product(): jnp.einsum('nab,bc->nac', field, matrix, preferred_element_type=jnp.float32)]
    dynamic_slice x66 -> x2, local copies, waits for them, and re-layouts: 38 us -> 0.1 us  [the longest x1 0.07 us: local(): lax.dynamic_slice_in_dim(offsets, section_no * per_batch, per_batch, 1)]
    all_gather x2 -> x1, waiting for transfers between devices: 30.9 us -> 0.01 us  [local(): lax.all_gather(encode(trans_real, trans_imag), 'cuts', axis=0, tiled=True)]
    all_to_all x0 -> x1, blocking collectives: none -> 29.5 us  [local(): lax.all_to_all(partial, 'cuts', split_axis=0, concat_axis=0, tiled=True)]
  transfers between devices with their start and end apart: 5 -> 4, of which waited for: 3 -> 3; matrix products, arithmetic and copies ran while one was open for 19% -> 5% of each run, Pallas kernels for 0% -> 0%
where the time goes in v1:
time: 126 us
  starting transfers between devices  29.6 us (23%)
  blocking collectives  29.5 us (23%)
  waiting for transfers between devices  28.4 us (23%)
  Pallas kernels  13.5 us (11%)
  between operations  13.5 us (11%)
  other arithmetic  7.26 us (6%)
  local copies, waits for them, and re-layouts  3.72 us (3%)
    all_to_all x1, blocking collectives, local(): lax.all_to_all(partial, 'cuts', split_axis=0, concat_axis=0, tiled=True)  29.5 us
    all_to_all x1, starting transfers between devices, fetch_patterns(): lax.all_to_all(request, 'tile', split_axis=0, concat_axis=0, tiled=True)  17.1 us
    pallas_call x1, Pallas kernels, patch_gradient(): pl.pallas_call(gradient_kernel, out_shape=jax.ShapeDtypeStruct((slices, 2...  13.5 us
    all_to_all x1, waiting for transfers between devices, fetch_patterns(): lax.all_to_all(jnp.take(mine, requested, axis=0), 'tile', split_axis=0, c...  12.4 us
    all_to_all x1, waiting for transfers between devices, fetch_patterns(): lax.all_to_all(request, 'tile', split_axis=0, concat_axis=0, tiled=True)  10.8 us
    all_to_all x1, starting transfers between devices, local(): lax.all_to_all(pieces.reshape(sections, per_batch, extent // sections, ex...  7.84 us
    all_to_all x1, waiting for transfers between devices, local(): lax.all_to_all(pieces.reshape(sections, per_batch, extent // sections, ex...  5.15 us
    all_to_all x1, starting transfers between devices, fetch_patterns(): lax.all_to_all(jnp.take(mine, requested, axis=0), 'tile', split_axis=0, c...  4.62 us
  transfers between devices with their start and end apart: 4, of which 3 were waited for; matrix products, arithmetic and copies ran while one was open for 5% of the time, Pallas kernels for 0%

profile of v1, /device:TPU:1, one launch (start us, length us, event | category | flops | bytes accessed | tf_op | source)
XLA Modules:
  0.0 125.5 jit_solution(17847235475647205675)
XLA Ops:
  6.5 0.0 copy-start
  6.5 0.0 copy-start.2
  6.5 0.0 copy-start.5
  6.5 0.0 copy-start.3
  6.5 0.0 copy-start.4
  6.5 0.0 all-gather.2.cloned.1.call-start
  6.6 1.9 %and_or_fusion = s32[1,256,256]{2,1,0:T(8,128)} fusion(f32[1,256,256]{2,1,0:T(8,128)} %param.9, f32[1,256,256]{2,1,0:T(8,128)} %param.8), kind=kLoop, calls=%fused_computation.3 | loop fusion | flops 655360 | bytes 786432 | tf_op jit(solution)/shard_map/or | solution.py:40
  8.5 0.0 all-gather.2.cloned.1.call-update
  8.5 0.7 and_select_fusion
  9.2 0.7 compare_and_fusion.1
  9.9 0.1 select_reduce_fusion
  9.9 0.7 copy.11
  10.6 17.1 %all-to-all-start = ((s32[64,1,1]{2,1,0:T(1,128)}), s32[64,1,1]{2,1,0:T(1,128)S(1)}, u32[]{:S(2)}, u32[]{:S(2)}) async-start(s32[64,1,1]{2,1,0:T(1,128)} %copy.11), calls=%async_computation | async-start | bytes 65536 | tf_op jit(solution)/shard_map/all_to_all | solution.py:203
  27.8 0.0 copy-done
  27.8 10.8 %all-to-all-done = s32[64,1,1]{2,1,0:T(1,128)S(1)} async-done(((s32[64,1,1]{2,1,0:T(1,128)}), s32[64,1,1]{2,1,0:T(1,128)S(1)}, u32[]{:S(2)}, u32[]{:S(2)}) %all-to-all-start) | async-done | bytes 288 | tf_op jit(solution)/shard_map/all_to_all | solution.py:203
  38.6 1.2 reduce
  39.9 0.6 gather_fusion
  40.5 0.8 broadcast_select_fusion
  41.4 4.6 %all-to-all-start.1 = ((bf16[64,16,128]{2,1,0:T(8,128)(2,1)}), bf16[64,16,128]{2,1,0:T(8,128)(2,1)S(1)}, u32[]{:S(2)}, u32[]{:S(2)}) async-start(bf16[64,16,128]{2,1,0:T(8,128)(2,1)} %broadcast_select_fusion), calls=%async_computation.1 | async-start | bytes 524288 | tf_op jit(solution)/shard_map/all_to_all | solution.py:205
  46.0 0.1 broadcast_in_dim.39
  46.1 12.4 %all-to-all-done.1 = bf16[64,16,128]{2,1,0:T(8,128)(2,1)S(1)} async-done(((bf16[64,16,128]{2,1,0:T(8,128)(2,1)}), bf16[64,16,128]{2,1,0:T(8,128)(2,1)S(1)}, u32[]{:S(2)}, u32[]{:S(2)}) %all-to-all-start.1) | async-done | bytes 262176 | tf_op jit(solution)/shard_map/all_to_all | solution.py:205
  58.5 0.6 gather_fusion.1
  59.1 0.8 broadcast_select_fusion.1
  59.9 7.8 %all-to-all-start.2 = ((bf16[8,4,16,128]{3,2,1,0:T(8,128)(2,1)}), bf16[8,4,16,128]{3,2,1,0:T(8,128)(2,1)S(1)}, u32[]{:S(2)}, u32[]{:S(2)}) async-start(bf16[8,4,16,128]{3,2,1,0:T(8,128)(2,1)} %broadcast_select_fusion.1), calls=%async_computation.2 | async-start | bytes 262144 | tf_op jit(solution)/shard_map/all_to_all | solution.py:220
  67.7 0.0 copy-done.5
  67.7 0.1 constant_dynamic-slice_fusion.1.offset_ref
  67.8 0.0 copy-done.3
  67.8 0.0 copy-done.4
  67.8 5.2 %all-to-all-done.2.amp_ref = bf16[8,4,16,128]{3,2,1,0:T(8,128)(2,1)S(1)} async-done(((bf16[8,4,16,128]{3,2,1,0:T(8,128)(2,1)}), bf16[8,4,16,128]{3,2,1,0:T(8,128)(2,1)S(1)}, u32[]{:S(2)}, u32[]{:S(2)}) %all-to-all-start.2) | async-done | bytes 131104 | tf_op jit(solution)/shard_map/all_to_all | solution.py:220
  72.9 0.0 all-gather.2.cloned.1.call-done.patch_ref
  72.9 0.0 copy-done.2
  72.9 0.0 copy-start.1
  72.9 1.6 %copy-done.1 = s32[8,256,256]{2,1,0:T(8,128)S(1)} copy-done((s32[8,256,256]{2,1,0:T(8,128)S(1)}, s32[8,256,256]{2,1,0:T(8,128)}, u32[]{:S(2)}) %copy-start.1) | copy-done | bytes 2097176
  74.5 13.5 %patch_gradient.1 = bf16[8,512,256]{2,1,0:T(8,128)(2,1)S(1)} custom-call(s32[2,4]{1,0:T(2,128)S(1)} %constant_dynamic-slice_fusion.1.offset_ref, s32[8,256,256]{2,1,0:T(8,128)S(1)} %copy-done.1, bf16[2,128,128]{2,1,0:T(8,128)(2,1)S(1)} %pad_maximum_fusion.probe_ref, bf16[8,4,16,128]{3,2,1,0:T(8,128)(2,1)S(1)} %all-to-all-done.2.amp_ref, ...), custom_call_target="tpu_custom_call" | custom-call | flops 2415919104 | bytes 6291456 | tf_op jit(solution)/shard_map/patch_gradient/pallas_call | solution.py:175
  88.1 29.5 %all_to_all.30 = bf16[8,512,256]{2,1,0:T(8,128)(2,1)S(1)} all-to-all(bf16[8,512,256]{2,1,0:T(8,128)(2,1)S(1)} %patch_gradient.1), channel_id=1, replica_groups=mesh['cuts'=8,'tile'=64] {'cuts'}, dimensions={0} | all-to-all | bytes 4194304 | tf_op jit(solution)/shard_map/all_to_all | solution.py:232
  117.6 1.1 convert_reduce_fusion
  (7 shorter events, 0.1 us)
Async XLA Ops:
  6.5 21.3 %copy-start = (bf16[32,128,128]{2,1,0:T(8,128)(2,1)S(1)}, bf16[32,128,128]{2,1,0:T(8,128)(2,1)}, u32[]{:S(2)}) copy-start(bf16[32,128,128]{2,1,0:T(8,128)(2,1)} %param.14) | copy-start | bytes 3145732
  6.5 66.4 %copy-start.2 = (bf16[4,256,256]{2,1,0:T(8,128)(2,1)S(1)}, bf16[4,256,256]{2,1,0:T(8,128)(2,1)}, u32[]{:S(2)}) copy-start(bf16[4,256,256]{2,1,0:T(8,128)(2,1)} %constant.82.clone.table_ref) | copy-start | bytes 1572868
  6.5 61.2 %copy-start.5 = (s32[2,32]{1,0:T(2,128)S(1)}, s32[2,32]{1,0:T(2,128)}, u32[]{:S(2)}) copy-start(s32[2,32]{1,0:T(2,128)} %param.12) | copy-start | bytes 772
  6.5 61.2 %copy-start.3 = (bf16[128,128]{1,0:T(8,128)(2,1)S(1)}, bf16[128,128]{1,0:T(8,128)(2,1)}, u32[]{:S(2)}) copy-start(bf16[128,128]{1,0:T(8,128)(2,1)} %param.11) | copy-start | bytes 98308
  6.5 61.2 %copy-start.4 = (bf16[128,128]{1,0:T(8,128)(2,1)S(1)}, bf16[128,128]{1,0:T(8,128)(2,1)}, u32[]{:S(2)}) copy-start(bf16[128,128]{1,0:T(8,128)(2,1)} %param.10) | copy-start | bytes 98308
  6.5 66.4 %all-gather.2.cloned.1.call-start = ((), (), s32[]{:S(2)}) async-start(), calls=%async_computation.4 | async-start | bytes 2359296 | tf_op jit(solution)/shard_map/all_gather | solution.py:227
  10.6 28.0 %all-to-all-start = ((s32[64,1,1]{2,1,0:T(1,128)}), s32[64,1,1]{2,1,0:T(1,128)S(1)}, u32[]{:S(2)}, u32[]{:S(2)}) async-start(s32[64,1,1]{2,1,0:T(1,128)} %copy.11), calls=%async_computation | async-start | bytes 65536 | tf_op jit(solution)/shard_map/all_to_all | solution.py:203
  41.4 17.1 %all-to-all-start.1 = ((bf16[64,16,128]{2,1,0:T(8,128)(2,1)}), bf16[64,16,128]{2,1,0:T(8,128)(2,1)S(1)}, u32[]{:S(2)}, u32[]{:S(2)}) async-start(bf16[64,16,128]{2,1,0:T(8,128)(2,1)} %broadcast_select_fusion), calls=%async_computation.1 | async-start | bytes 524288 | tf_op jit(solution)/shard_map/all_to_all | solution.py:205
  59.9 13.1 %all-to-all-start.2 = ((bf16[8,4,16,128]{3,2,1,0:T(8,128)(2,1)}), bf16[8,4,16,128]{3,2,1,0:T(8,128)(2,1)S(1)}, u32[]{:S(2)}, u32[]{:S(2)}) async-start(bf16[8,4,16,128]{3,2,1,0:T(8,128)(2,1)} %broadcast_select_fusion.1), calls=%async_computation.2 | async-start | bytes 262144 | tf_op jit(solution)/shard_map/all_to_all | solution.py:220
  72.9 1.6 %copy-start.1 = (s32[8,256,256]{2,1,0:T(8,128)S(1)}, s32[8,256,256]{2,1,0:T(8,128)}, u32[]{:S(2)}) copy-start(s32[8,256,256]{2,1,0:T(8,128)} %all-gather.2.cloned.1.call-done.patch_ref) | copy-start | bytes 6291460
Sparse Core Ops, SparseCore 0:
  9.5 36.4 all-gather.1

commit v2 on v1

--- a/solution.py
+++ b/solution.py
@@ -8,6 +8,7 @@
 from jax.experimental import pallas as pl
 from jax.experimental.pallas import tpu as pltpu
 from jax.sharding import PartitionSpec as P
+
 
 fresnel_strength = 9.0
 softening = 0.01
@@ -68,37 +69,52 @@
     )
 
 
-def gradient_kernel(
-    offset_ref, patch_ref, probe_ref, amp_ref, table_ref, out_ref, code_ref, wave_ref, grad_ref, sum_ref
+def placed(offset_ref, position, side, tall):
+    row_at = offset_ref[0, position]
+    start = jnp.minimum(row_at // 8, (side - tall) // 8) * 8
+    return pl.multiple_of(start, 8), row_at - start
+
+
+def part(extent, pair, item):
+    return pair * 2 + item, slice(item * extent, (item + 1) * extent)
+
+
+def descend_kernel(
+    offset_ref, order_ref, table_hbm, probe_ref, *refs
 ):
-    slices, side, _ = patch_ref.shape
-    extent = probe_ref.shape[1]
-    count = code_ref.shape[1]
+    patches_hbm = refs[:-12]
+    codes_hbm, waves_hbm, far_hbm = refs[-12:-9]
+    table_ref, patch_ref, code_ref, wave_ref, far_ref, table_sem, patch_sem, code_sem, wave_sem = refs[-9:]
+    slices, count, extent, _ = code_ref.shape
+    side = patch_ref.shape[-1]
     pairs = count // 2
-    pieces, _, piece_rows, _ = amp_ref.shape
-
     tall = extent + 8
 
-    def placed(position):
-        row_at = offset_ref[0, position]
-        start = jnp.minimum(row_at // 8, (side - tall) // 8) * 8
-        return pl.multiple_of(start, 8), row_at - start
-
-    def part(pair, item):
-        return pair * 2 + item, slice(item * extent, (item + 1) * extent)
-
+    table_in = pltpu.make_async_copy(table_hbm, table_ref, table_sem)
+    table_in.start()
+    for place, hbm in enumerate(patches_hbm):
+        layer = order_ref[place]
+        pltpu.make_async_copy(hbm.at[0], patch_ref.at[layer], patch_sem.at[layer]).start()
     for pair in range(pairs):
         for item in range(2):
-            _, rows = part(pair, item)
+            _, rows = part(extent, pair, item)
             wave_ref[0, pair, rows, :extent] = probe_ref[0]
             wave_ref[0, pair, rows, extent:] = probe_ref[1]
+    table_in.wait()
+
+    def code_out(layer):
+        return pltpu.make_async_copy(code_ref.at[layer], codes_hbm.at[layer], code_sem.at[layer])
+
+    def wave_out(layer):
+        return pltpu.make_async_copy(wave_ref.at[layer], waves_hbm.at[layer - 1], wave_sem.at[layer])
 
     def descend(layer, carry):
+        pltpu.make_async_copy(patches_hbm[0].at[0], patch_ref.at[layer], patch_sem.at[layer]).wait()
         for pair in range(pairs):
             fields = []
             for item in range(2):
-                position, rows = part(pair, item)
-                row_at, down = placed(position)
+                position, rows = part(extent, pair, item)
+                row_at, down = placed(offset_ref, position, side, tall)
                 back = lax.rem(side - offset_ref[1, position], side)
                 code = pltpu.roll(patch_ref[layer, pl.ds(row_at, tall), :], back, 1)[:, :extent]
                 code = pltpu.roll(code, lax.rem(tall - down, tall), 0)[:extent]
@@ -113,16 +129,82 @@
                 )
             ahead = both_sides(table_ref[0], table_ref[1], jnp.concatenate(fields, axis=0))
             wave_ref[layer + 1, pair] = ahead.astype(jnp.bfloat16)
+        code_out(layer).start()
+
+        @pl.when(layer < slices - 1)
+        def _():
+            wave_out(layer + 1).start()
+
         return carry
 
     lax.fori_loop(0, slices, descend, 0)
-
     for pair in range(pairs):
-        far = both_sides(table_ref[2], table_ref[3], wave_ref[slices, pair])
+        far_ref[pair] = both_sides(table_ref[2], table_ref[3], wave_ref[slices, pair])
+    far_out = pltpu.make_async_copy(far_ref, far_hbm, table_sem)
+    far_out.start()
+    for layer in range(slices):
+        code_out(layer).wait()
+        if layer > 0:
+            wave_out(layer).wait()
+    far_out.wait()
+
+
+def ascend_kernel(
+    offset_ref,
+    core_ref,
+    table_hbm,
+    probe_ref,
+    amp_ref,
+    codes_hbm,
+    waves_hbm,
+    far_hbm,
+    own_ref,
+    other_ref,
+    table_ref,
+    code_ref,
+    wave_ref,
+    far_ref,
+    grad_ref,
+    sum_ref,
+    table_sem,
+    far_sem,
+    code_sem,
+    wave_sem,
+):
+    slices, count, extent, _ = code_ref.shape
+    side = own_ref.shape[-1]
+    pairs = count // 2
+    pieces = amp_ref.shape[0]
+    tall = extent + 8
+
+    far_in = pltpu.make_async_copy(far_hbm, far_ref, far_sem)
+    far_in.start()
+    table_in = pltpu.make_async_copy(table_hbm, table_ref, table_sem)
+    table_in.start()
+
+    def code_in(layer):
+        return pltpu.make_async_copy(codes_hbm.at[layer], code_ref.at[layer], code_sem.at[layer])
+
+    def wave_in(layer):
+        return pltpu.make_async_copy(waves_hbm.at[layer - 1], wave_ref.at[layer], wave_sem.at[layer])
+
+    for layer in reversed(range(slices)):
+        code_in(layer).start()
+        if layer > 0:
+            wave_in(layer).start()
+    for pair in range(pairs):
+        for item in range(2):
+            _, rows = part(extent, pair, item)
+            wave_ref[0, pair, rows, :extent] = probe_ref[0]
+            wave_ref[0, pair, rows, extent:] = probe_ref[1]
+    far_in.wait()
+    table_in.wait()
+
+    for pair in range(pairs):
         residue = []
         for item in range(2):
-            position, rows = part(pair, item)
-            f_real, f_imag = far[rows, :extent], far[rows, extent:]
+            position, rows = part(extent, pair, item)
+            f_real, f_imag = far_ref[pair, rows, :extent], far_ref[pair, rows, extent:]
             amplitude = jnp.concatenate(
                 [amp_ref[piece, position] for piece in range(pieces)], axis=0
             ).astype(jnp.float32)
@@ -136,18 +218,24 @@
 
     def ascend(step, carry):
         layer = slices - 1 - step
+        code_in(layer).wait()
+
+        @pl.when(layer > 0)
+        def _():
+            wave_in(layer).wait()
+
         sum_ref[...] = jnp.zeros_like(sum_ref)
         for pair in range(pairs):
             back = both_sides(table_ref[1], table_ref[0], grad_ref[pair])
             for item in range(2):
-                position, rows = part(pair, item)
+                position, rows = part(extent, pair, item)
                 u_real, u_imag = back[rows, :extent], back[rows, extent:]
                 t_real, t_imag = decode(code_ref[layer, position])
                 grad_ref[pair, rows, :extent] = (u_real * t_real + u_imag * t_imag).astype(jnp.bfloat16)
                 grad_ref[pair, rows, extent:] = (u_imag * t_real - u_real * t_imag).astype(jnp.bfloat16)
                 wave = wave_ref[layer, pair, rows, :].astype(jnp.float32)
                 w_real, w_imag = wave[:, :extent], wave[:, extent:]
-                row_at, down = placed(position)
+                row_at, down = placed(offset_ref, position, side, tall)
                 col_at = offset_ref[1, position]
                 for plane, contrib in enumerate(
                     (u_real * w_real + u_imag * w_imag, u_imag * w_real - u_real * w_imag)
@@ -160,41 +248,96 @@
                         axis=1,
                     )
                     sum_ref[plane, pl.ds(row_at, tall), :] += pltpu.roll(wide, col_at, 1)
-        out_ref[layer, :side] = sum_ref[0].astype(jnp.bfloat16)
-        out_ref[layer, side:] = sum_ref[1].astype(jnp.bfloat16)
+        mine = layer % 2 == core_ref[0]
+
+        @pl.when(mine)
+        def _():
+            own_ref[layer // 2, :side] = sum_ref[0].astype(jnp.bfloat16)
+            own_ref[layer // 2, side:] = sum_ref[1].astype(jnp.bfloat16)
+
+        @pl.when(jnp.logical_not(mine))
+        def _():
+            other_ref[layer // 2, :side] = sum_ref[0].astype(jnp.bfloat16)
+            other_ref[layer // 2, side:] = sum_ref[1].astype(jnp.bfloat16)
+
         return carry
 
     lax.fori_loop(0, slices, ascend, 0)
 
 
-def patch_gradient(offset_mine, patches, probe, amp_pieces, table):
-    slices, side, _ = patches.shape
+SMEM = pl.BlockSpec(memory_space=pltpu.SMEM)
+VMEM = pl.BlockSpec(memory_space=pltpu.VMEM)
+HBM = pl.BlockSpec(memory_space=pltpu.HBM)
+FULL = 67_043_328
+PARAMS = pltpu.CompilerParams(vmem_limit_bytes=FULL - (1 << 19))
+
+
+def forward(offset_mine, order, patches, probe, table):
+    slices = len(patches)
+    side = patches[0].shape[-1]
     extent = probe.shape[-1]
     count = offset_mine.shape[1]
-    vmem = pl.BlockSpec(memory_space=pltpu.VMEM)
+    square = (count // 2, 2 * extent, 2 * extent)
     return pl.pallas_call(
-        gradient_kernel,
-        out_shape=jax.ShapeDtypeStruct((slices, 2 * side, side), jnp.bfloat16),
-        in_specs=[pl.BlockSpec(memory_space=pltpu.SMEM), vmem, vmem, vmem, vmem],
-        out_specs=vmem,
+        descend_kernel,
+        out_shape=(
+            jax.ShapeDtypeStruct((slices, count, extent, extent), jnp.int32),
+            jax.ShapeDtypeStruct((slices - 1,) + square, jnp.bfloat16),
+            jax.ShapeDtypeStruct(square, jnp.float32),
+        ),
+        in_specs=[SMEM, SMEM, HBM, VMEM] + [HBM] * slices,
+        out_specs=(HBM, HBM, HBM),
         scratch_shapes=[
+            pltpu.VMEM(table.shape, table.dtype),
+            pltpu.VMEM((slices, side, side), jnp.int32),
             pltpu.VMEM((slices, count, extent, extent), jnp.int32),
-            pltpu.VMEM((slices + 1, count // 2, 2 * extent, 2 * extent), jnp.bfloat16),
-            pltpu.VMEM((count // 2, 2 * extent, 2 * extent), jnp.bfloat16),
+            pltpu.VMEM((slices + 1,) + square, jnp.bfloat16),
+            pltpu.VMEM(square, jnp.float32),
+            pltpu.SemaphoreType.DMA,
+            pltpu.SemaphoreType.DMA((slices,)),
+            pltpu.SemaphoreType.DMA((slices,)),
+            pltpu.SemaphoreType.DMA((slices,)),
+        ],
+        name="descend",
+        compiler_params=PARAMS,
+        cost_estimate=pl.CostEstimate(
+            flops=2 * (slices + 1) * count * 8 * extent**3, bytes_accessed=6 << 20, transcendentals=0
+        ),
+    )(offset_mine, order, table, probe, *patches)
+
+
+def backward(offset_mine, core, table, probe, amp_pieces, codes, waves, far, side):
+    slices, count, extent, _ = codes.shape
+    half = jax.ShapeDtypeStruct((slices // 2, 2 * side, side), jnp.bfloat16)
+    square = (count // 2, 2 * extent, 2 * extent)
+    return pl.pallas_call(
+        ascend_kernel,
+        out_shape=(half, half),
+        in_specs=[SMEM, SMEM, HBM, VMEM, VMEM, HBM, HBM, HBM],
+        out_specs=(VMEM, VMEM),
+        scratch_shapes=[
+            pltpu.VMEM(table.shape, table.dtype),
+            pltpu.VMEM((slices, count, extent, extent), jnp.int32),
+            pltpu.VMEM((slices,) + square, jnp.bfloat16),
+            pltpu.VMEM(square, jnp.float32),
+            pltpu.VMEM(square, jnp.bfloat16),
             pltpu.VMEM((2, side, side), jnp.float32),
+            pltpu.SemaphoreType.DMA,
+            pltpu.SemaphoreType.DMA,
+            pltpu.SemaphoreType.DMA((slices,)),
+            pltpu.SemaphoreType.DMA((slices,)),
         ],
-        name="patch_gradient",
-        compiler_params=pltpu.CompilerParams(vmem_limit_bytes=40 << 20),
+        name="ascend",
+        compiler_params=pltpu.CompilerParams(vmem_limit_bytes=FULL - (5 << 19)),
         cost_estimate=pl.CostEstimate(
-            flops=2 * (slices + 1) * 2 * count * 8 * extent**3, bytes_accessed=6 << 20, transcendentals=0
+            flops=2 * (slices + 1) * count * 8 * extent**3, bytes_accessed=6 << 20, transcendentals=0
         ),
-    )(offset_mine, patches, probe, amp_pieces, table)
+    )(offset_mine, core, table, probe, amp_pieces, codes, waves, far)
 
 
 def fetch_patterns(pattern_index, measured, section_no, sections):
-    positions = pattern_index.shape[0]
+    positions, extent, _ = measured.shape
     tile_count = lax.axis_size("tile")
-    extent = measured.shape[1]
     share = extent // sections
     owners = pattern_index // positions
     slots = pattern_index % positions
@@ -202,10 +345,15 @@
     request = jnp.sum(jnp.where(named, slots[None, :], 0), axis=1)
     requested = lax.all_to_all(request, "tile", split_axis=0, concat_axis=0, tiled=True)
     mine = lax.dynamic_slice_in_dim(measured, section_no * share, share, 1)
-    answered = lax.all_to_all(
-        jnp.take(mine, requested, axis=0), "tile", split_axis=0, concat_axis=0, tiled=True
-    )
-    return jnp.take(answered, owners, axis=0)
+    rows = mine.at[requested].get(mode="promise_in_bounds")
+    answered = lax.all_to_all(rows, "tile", split_axis=0, concat_axis=0, tiled=True)
+    pieces = answered.at[owners].get(mode="promise_in_bounds")
+    pieces = pieces.reshape(sections, positions // sections, share, extent)
+    return lax.all_to_all(pieces, "cuts", split_axis=0, concat_axis=0, tiled=True)
+
+
+def across(chips, step):
+    return [(2 * at + core, 2 * ((at + step) % chips) + core) for at in range(chips) for core in range(2)]
 
 
 def local(trans_real, trans_imag, probe_real, probe_imag, offsets, pattern_index, measured):
@@ -215,21 +363,31 @@
     sections = lax.axis_size("cuts")
     section_no = lax.axis_index("cuts")
     per_batch = positions // sections
+    chips = sections // 2
+    chip, core = section_no // 2, section_no % 2
+    sibling = [(at, at ^ 1) for at in range(sections)]
+    steps = sorted(range(1, chips), key=lambda step: min(step, chips - step))
+
     table = jnp.asarray(tables(extent))
-    pieces = fetch_patterns(pattern_index, measured, section_no, sections)
-    amp_pieces = lax.all_to_all(
-        pieces.reshape(sections, per_batch, extent // sections, extent),
-        "cuts",
-        split_axis=0,
-        concat_axis=0,
-        tiled=True,
+    probe = jnp.stack([probe_real, probe_imag])
+    offset_mine = lax.dynamic_slice_in_dim(offsets, section_no * per_batch, per_batch, 1)
+    amp_pieces = fetch_patterns(pattern_index, measured, section_no, sections)
+    code = encode(trans_real, trans_imag)
+    patches = [code] + [lax.ppermute(code, "cuts", across(chips, step)) for step in steps]
+    near = [lax.ppermute(code, "cuts", sibling)]
+    near += [lax.ppermute(patch, "cuts", sibling) for patch in patches[1:]]
+    came = (chip - jnp.array([0] + steps, jnp.int32)) % chips * 2
+    order = jnp.concatenate([came + core, came + 1 - core])
+    codes, waves, far = forward(offset_mine, order, patches + near, probe, table)
+    own, other = backward(
+        offset_mine, core[None], table, probe, amp_pieces, codes, waves, far, side
     )
-    patches = lax.all_gather(encode(trans_real, trans_imag), "cuts", axis=0, tiled=True)
-    offset_mine = lax.dynamic_slice_in_dim(offsets, section_no * per_batch, per_batch, 1)
-    partial = patch_gradient(
-        offset_mine, patches, jnp.stack([probe_real, probe_imag]), amp_pieces, table
+    met = lax.ppermute(other, "cuts", sibling)
+    paired = (own.astype(jnp.float32) + met.astype(jnp.float32)).astype(jnp.bfloat16)
+    groups = [[2 * at + parity for at in range(chips)] for parity in range(2)]
+    parts = lax.all_to_all(
+        paired, "cuts", split_axis=0, concat_axis=0, tiled=True, axis_index_groups=groups
     )
-    parts = lax.all_to_all(partial, "cuts", split_axis=0, concat_axis=0, tiled=True)
     total = jnp.sum(parts.astype(jnp.float32), axis=0)
     return total.reshape(2, 1, side, side)
 

time: 126 us -> 122 us (0.968)
  starting transfers between devices: 29.6 us -> 51.5 us
  between operations: 13.5 us -> 0.28 us
  waiting for transfers between devices: 28.4 us -> 15.4 us
  blocking collectives: 29.5 us -> 18.3 us
  Pallas kernels: 13.5 us -> 20.9 us
  local copies, waits for them, and re-layouts: 3.72 us -> 6.99 us
    ppermute x0 -> x8, starting transfers between devices: none -> 27.4 us  [the longest x3 10.8 us: local(): lax.ppermute(code, 'cuts', across(chips, step))]
    all_to_all x2, waiting for transfers between devices: 17.6 us -> 3.43 us  [the longest x1 3.43 us: fetch_patterns(): lax.all_to_all(rows, 'tile', split_axis=0, concat_axis=0, tiled=True)]
    all_to_all x1, blocking collectives: 29.5 us -> 18.3 us  [local(): lax.all_to_all(paired, 'cuts', split_axis=0, concat_axis=0, tiled=True, a...]
    pallas_call x1 -> x2, Pallas kernels: 13.5 us -> 20.9 us  [the longest x1 11.6 us: backward(): pl.pallas_call(ascend_kernel, out_shape=(half, half), in_specs=[SMEM, SME...]
    all_to_all x1, starting transfers between devices: 17.1 us -> 12.8 us  [fetch_patterns(): lax.all_to_all(request, 'tile', split_axis=0, concat_axis=0, tiled=True)]
    ppermute x0 -> x8, waiting for transfers between devices: none -> 2.75 us  [the longest x1 2.73 us: local(): met = lax.ppermute(other, 'cuts', sibling)]
    all_to_all x1, waiting for transfers between devices: 10.8 us -> 9.19 us  [fetch_patterns(): lax.all_to_all(request, 'tile', split_axis=0, concat_axis=0, tiled=True)]
    select_n x5 -> x2, other arithmetic: 2.26 us -> 0.68 us  [the longest x1 0.67 us: fetch_patterns(): pieces = answered.at[owners].get(mode='promise_in_bounds')]
  transfers between devices with their start and end apart: 4 -> 11, of which waited for: 3 -> 3; matrix products, arithmetic and copies ran while one was open for 5% -> 7% of each run, Pallas kernels for 0% -> 8%
where the time goes in v2:
time: 122 us; the launch traced here: 121 us
  starting transfers between devices  51.5 us (42%)
  Pallas kernels  20.9 us (17%)
  blocking collectives  18.3 us (15%)
  waiting for transfers between devices  15.4 us (13%)
  other arithmetic  7.49 us (6%)
  local copies, waits for them, and re-layouts  6.99 us (6%)
    all_to_all x1, blocking collectives, local(): lax.all_to_all(paired, 'cuts', split_axis=0, concat_axis=0, tiled=True, a...  18.3 us
    all_to_all x1, starting transfers between devices, fetch_patterns(): lax.all_to_all(request, 'tile', split_axis=0, concat_axis=0, tiled=True)  12.8 us
    pallas_call x1, Pallas kernels, backward(): pl.pallas_call(ascend_kernel, out_shape=(half, half), in_specs=[SMEM, SME...  11.6 us
    ppermute x3, starting transfers between devices, local(): lax.ppermute(code, 'cuts', across(chips, step))  10.8 us
    pallas_call x1, Pallas kernels, forward(): pl.pallas_call(descend_kernel, out_shape=(jax.ShapeDtypeStruct((slices, c...  9.38 us
    all_to_all x1, waiting for transfers between devices, fetch_patterns(): lax.all_to_all(request, 'tile', split_axis=0, concat_axis=0, tiled=True)  9.19 us
    ppermute x3, starting transfers between devices, local(): near += [lax.ppermute(patch, 'cuts', sibling) for patch in patches[1:]]  7.69 us
    ppermute x1, starting transfers between devices, local(): near = [lax.ppermute(code, 'cuts', sibling)]  6.96 us
  transfers between devices with their start and end apart: 11, of which 3 were waited for; matrix products, arithmetic and copies ran while one was open for 7% of the time, Pallas kernels for 8%

profile of v2, /device:TPU:1, one launch (start us, length us, event | category | flops | bytes accessed | tf_op | source)
XLA Modules:
  0.0 120.9 jit_solution(15241844006367254306)
XLA Ops:
  0.0 0.0 copy-start
  0.0 1.1 and_or_fusion.refs_0_
  1.1 0.0 copy-start.2
  1.1 3.9 %collective-permute-start = (s32[1,256,256]{2,1,0:T(8,128)S(1)}, s32[1,256,256]{2,1,0:T(8,128)S(1)}, u32[]{:S(2)}, u32[]{:S(2)}) collective-permute-start(s32[1,256,256]{2,1,0:T(8,128)S(1)} %and_or_fusion.refs_0_), channel_id=1, source_target_pairs={{0,128},{64,192},{128,256},{192,320},{256,384},{320,448},{384,0},{... | collective-permute-start | bytes 786440 | tf_op jit(solution)/shard_map/ppermute | solution.py:376
  5.1 3.2 %collective-permute-start.1 = (s32[1,256,256]{2,1,0:T(8,128)S(1)}, s32[1,256,256]{2,1,0:T(8,128)S(1)}, u32[]{:S(2)}, u32[]{:S(2)}) collective-permute-start(s32[1,256,256]{2,1,0:T(8,128)S(1)} %and_or_fusion.refs_0_), channel_id=1, source_target_pairs={{0,384},{64,448},{128,0},{192,64},{256,128},{320,192},{384,256},{4... | collective-permute-start | bytes 786440 | tf_op jit(solution)/shard_map/ppermute | solution.py:376
  8.3 3.6 %collective-permute-start.2 = (s32[1,256,256]{2,1,0:T(8,128)S(1)}, s32[1,256,256]{2,1,0:T(8,128)S(1)}, u32[]{:S(2)}, u32[]{:S(2)}) collective-permute-start(s32[1,256,256]{2,1,0:T(8,128)S(1)} %and_or_fusion.refs_0_), channel_id=1, source_target_pairs={{0,256},{64,320},{128,384},{192,448},{256,0},{320,64},{384,128},{4... | collective-permute-start | bytes 786440 | tf_op jit(solution)/shard_map/ppermute | solution.py:376
  11.9 7.0 %collective-permute-start.3 = (s32[1,256,256]{2,1,0:T(8,128)S(1)}, s32[1,256,256]{2,1,0:T(8,128)S(1)}, u32[]{:S(2)}, u32[]{:S(2)}) collective-permute-start(s32[1,256,256]{2,1,0:T(8,128)S(1)} %and_or_fusion.refs_0_), channel_id=1, source_target_pairs={{0,64},{64,0},{128,192},{192,128},{256,320},{320,256},{384,448},{4... | collective-permute-start | bytes 786440 | tf_op jit(solution)/shard_map/ppermute | solution.py:377
  18.9 0.7 compare_select_fusion
  19.6 0.1 select_reduce_fusion
  19.6 0.7 copy.12
  20.4 12.8 %all-to-all-start = ((s32[64,1,1]{2,1,0:T(1,128)}), s32[64,1,1]{2,1,0:T(1,128)S(1)}, u32[]{:S(2)}, u32[]{:S(2)}) async-start(s32[64,1,1]{2,1,0:T(1,128)} %copy.12), calls=%async_computation | async-start | bytes 65536 | tf_op jit(solution)/shard_map/all_to_all | solution.py:346
  33.2 0.7 broadcast_add_fusion
  33.8 0.9 constant_dynamic-slice_fusion
  34.8 9.2 %all-to-all-done = s32[64,1,1]{2,1,0:T(1,128)S(1)} async-done(((s32[64,1,1]{2,1,0:T(1,128)}), s32[64,1,1]{2,1,0:T(1,128)S(1)}, u32[]{:S(2)}, u32[]{:S(2)}) %all-to-all-start) | async-done | bytes 288 | tf_op jit(solution)/shard_map/all_to_all | solution.py:346
  43.9 1.2 %reduce = s32[64]{0:T(128)S(1)} reduce(s32[64,1,1]{2,1,0:T(1,128)S(1)} %all-to-all-done, s32[]{:T(128)} %constant.78.clone.1), dimensions={1,2}, to_apply=%all_to_all.18.reduce_sub_computation | reduce | bytes 516 | tf_op jit(solution)/shard_map/all_to_all | solution.py:346
  45.2 1.3 %gather_fusion = bf16[64,16,128]{2,1,0:T(8,128)(2,1)} fusion(bf16[32,16,128]{2,1,0:T(8,128)(2,1)S(1)} %constant_dynamic-slice_fusion, s32[1024]{0:T(1024)S(1)} %pad_clamp_fusion.1), kind=kCustom, calls=%fused_computation | custom fusion | bytes 524544 | tf_op jit(solution)/shard_map/gather | solution.py:348
  46.5 4.6 %all-to-all-start.1 = ((bf16[64,16,128]{2,1,0:T(8,128)(2,1)}), bf16[64,16,128]{2,1,0:T(8,128)(2,1)S(1)}, u32[]{:S(2)}, u32[]{:S(2)}) async-start(bf16[64,16,128]{2,1,0:T(8,128)(2,1)} %gather_fusion), calls=%async_computation.1 | async-start | bytes 524288 | tf_op jit(solution)/shard_map/all_to_all | solution.py:349
  51.2 0.0 collective-permute-done.refs_1_
  51.2 0.0 copy-start.5
  51.2 3.4 %collective-permute-start.4 = (s32[1,256,256]{2,1,0:T(8,128)S(1)}, s32[1,256,256]{2,1,0:T(8,128)S(1)}, u32[]{:S(2)}, u32[]{:S(2)}) collective-permute-start(s32[1,256,256]{2,1,0:T(8,128)S(1)} %collective-permute-done.refs_1_), channel_id=1, source_target_pairs={{0,64},{64,0},{128,192},{192,128},{256,320},{320,256},{384,448},{4... | collective-permute-start | bytes 786440 | tf_op jit(solution)/shard_map/ppermute | solution.py:378
  54.6 0.0 collective-permute-done.1.refs_2_
  54.6 1.9 %collective-permute-start.5 = (s32[1,256,256]{2,1,0:T(8,128)S(1)}, s32[1,256,256]{2,1,0:T(8,128)S(1)}, u32[]{:S(2)}, u32[]{:S(2)}) collective-permute-start(s32[1,256,256]{2,1,0:T(8,128)S(1)} %collective-permute-done.1.refs_2_), channel_id=1, source_target_pairs={{0,64},{64,0},{128,192},{192,128},{256,320},{320,256},{384,448},{4... | collective-permute-start | bytes 786440 | tf_op jit(solution)/shard_map/ppermute | solution.py:378
  56.5 0.0 collective-permute-done.2.refs_3_
  56.5 2.4 %collective-permute-start.6 = (s32[1,256,256]{2,1,0:T(8,128)S(1)}, s32[1,256,256]{2,1,0:T(8,128)}, u32[]{:S(2)}, u32[]{:S(2)}) collective-permute-start(s32[1,256,256]{2,1,0:T(8,128)S(1)} %collective-permute-done.2.refs_3_), channel_id=1, source_target_pairs={{0,64},{64,0},{128,192},{192,128},{256,320},{320,256},{384,448},{4... | collective-permute-start | bytes 786440 | tf_op jit(solution)/shard_map/ppermute | solution.py:378
  59.0 0.6 constant_dynamic-slice_fusion.1.offset_ref
  59.6 0.6 pad_maximum_fusion.probe_ref
  60.2 3.4 %all-to-all-done.1 = bf16[64,16,128]{2,1,0:T(8,128)(2,1)S(1)} async-done(((bf16[64,16,128]{2,1,0:T(8,128)(2,1)}), bf16[64,16,128]{2,1,0:T(8,128)(2,1)S(1)}, u32[]{:S(2)}, u32[]{:S(2)}) %all-to-all-start.1) | async-done | bytes 262176 | tf_op jit(solution)/shard_map/all_to_all | solution.py:349
  63.7 1.2 %gather_fusion.1 = bf16[32,16,128]{2,1,0:T(8,128)(2,1)} fusion(bf16[64,16,128]{2,1,0:T(8,128)(2,1)S(1)} %all-to-all-done.1, s32[1024]{0:T(1024)S(1)} %pad_clamp_fusion), kind=kCustom, calls=%fused_computation.1 | custom fusion | bytes 262272 | tf_op jit(solution)/shard_map/gather | solution.py:350
  64.9 6.7 %all-to-all-start.2 = ((bf16[8,4,16,128]{3,2,1,0:T(8,128)(2,1)}), bf16[8,4,16,128]{3,2,1,0:T(8,128)(2,1)S(1)}, u32[]{:S(2)}, u32[]{:S(2)}) async-start(bf16[8,4,16,128]{3,2,1,0:T(8,128)(2,1)} %bitcast.5), calls=%async_computation.2 | async-start | bytes 262144 | tf_op jit(solution)/shard_map/all_to_all | solution.py:352
  71.6 0.6 pad_add_fusion.order_ref
  72.2 0.0 collective-permute-done.3.refs_4_
  72.2 0.0 copy-done.5
  72.2 0.0 collective-permute-done.4.refs_5_
  72.3 0.0 collective-permute-done.5.refs_6_
  72.3 0.0 copy-done.7
  72.3 0.7 copy-done.8
  72.9 0.1 copy-done.9
  73.1 0.7 copy-done.10
  73.8 0.0 collective-permute-done.6.refs_7_
  73.8 9.4 %descend.1 = (s32[8,4,128,128]{3,2,1,0:T(8,128)}, bf16[7,2,256,256]{3,2,1,0:T(8,128)(2,1)}, f32[2,256,256]{2,1,0:T(8,128)}) custom-call(s32[2,4]{1,0:T(2,128)} %constant_dynamic-slice_fusion.1.offset_ref, s32[8]{0:T(128)} %pad_add_fusion.order_ref, bf16[4,256,256]{2,1,0:T(8,128)(2,1)} %constant.97.clone.table_hbm, ...), custom_call_target="tpu_custom_call" | custom-call | flops 1207959552 | bytes 6291456 | tf_op jit(solution)/shard_map/descend/pallas_call | solution.py:281
  83.2 0.0 all-to-all-done.2.amp_ref
  83.2 0.6 copy-done.1
  83.8 11.6 %ascend.1 = (bf16[4,512,256]{2,1,0:T(8,128)(2,1)}, bf16[4,512,256]{2,1,0:T(8,128)(2,1)}) custom-call(s32[2,4]{1,0:T(2,128)} %constant_dynamic-slice_fusion.1.offset_ref, s32[1]{0:T(128)} %bitcast.core_ref, bf16[4,256,256]{2,1,0:T(8,128)(2,1)} %constant.97.clone.table_hbm, bf16[2,128,128]{2,1,0:T(8,128)(2,1)} %pad_maximum_fusion.probe_ref, ...), custom_call_target="tpu_custom_call" | custom-call | flops 1207959552 | bytes 6291456 | tf_op jit(solution)/shard_map/ascend/pallas_call | solution.py:313
  95.4 2.0 %collective-permute-start.7 = (bf16[4,512,256]{2,1,0:T(8,128)(2,1)}, bf16[4,512,256]{2,1,0:T(8,128)(2,1)S(1)}, u32[]{:S(2)}, u32[]{:S(2)}) collective-permute-start(bf16[4,512,256]{2,1,0:T(8,128)(2,1)} %get-tuple-element.14), channel_id=1, source_target_pairs={{0,64},{64,0},{128,192},{192,128},{256,320},{320,256},{384,448},{4... | collective-permute-start | bytes 3145736 | tf_op jit(solution)/shard_map/ppermute | solution.py:385
  97.4 2.7 %collective-permute-done.7 = bf16[4,512,256]{2,1,0:T(8,128)(2,1)S(1)} collective-permute-done((bf16[4,512,256]{2,1,0:T(8,128)(2,1)}, bf16[4,512,256]{2,1,0:T(8,128)(2,1)S(1)}, u32[]{:S(2)}, u32[]{:S(2)}) %collective-permute-start.7) | collective-permute-done | bytes 1048608 | tf_op jit(solution)/shard_map/ppermute | solution.py:385
  100.2 1.5 %add_convert_fusion = bf16[4,512,256]{2,1,0:T(8,128)(2,1)S(1)} fusion(bf16[4,512,256]{2,1,0:T(8,128)(2,1)S(1)} %collective-permute-done.7, bf16[4,512,256]{2,1,0:T(8,128)(2,1)} %get-tuple-element.13), kind=kLoop, calls=%fused_computation.3 | loop fusion | flops 2097152 | bytes 3145728 | tf_op jit(solution)/shard_map/convert_element_type | solution.py:386
  101.7 18.3 %all_to_all.27 = bf16[4,512,256]{2,1,0:T(8,128)(2,1)S(1)} all-to-all(bf16[4,512,256]{2,1,0:T(8,128)(2,1)S(1)} %add_convert_fusion), channel_id=1, replica_groups={{0,128,256,384},{64,192,320,448},{1,129,257,385},{65,193,321,449},{2,13..., dimensions={0} | all-to-all | bytes 2097152 | tf_op jit(solution)/shard_map/all_to_all | solution.py:388
  120.0 0.9 convert_reduce_fusion
  (17 shorter events, 0.0 us)
Async XLA Ops:
  0.0 58.9 %copy-start = (s32[2,32]{1,0:T(2,128)S(1)}, s32[2,32]{1,0:T(2,128)}, u32[]{:S(2)}) copy-start(s32[2,32]{1,0:T(2,128)} %param.13) | copy-start | bytes 772
  0.0 59.6 %copy-start.4 = (bf16[128,128]{1,0:T(8,128)(2,1)S(1)}, bf16[128,128]{1,0:T(8,128)(2,1)}, u32[]{:S(2)}) copy-start(bf16[128,128]{1,0:T(8,128)(2,1)} %param.11) | copy-start | bytes 98308
  0.0 59.6 %copy-start.3 = (bf16[128,128]{1,0:T(8,128)(2,1)S(1)}, bf16[128,128]{1,0:T(8,128)(2,1)}, u32[]{:S(2)}) copy-start(bf16[128,128]{1,0:T(8,128)(2,1)} %param.12) | copy-start | bytes 98308
  1.1 72.6 %copy-start.2 = (s32[1,256,256]{2,1,0:T(8,128)}, s32[1,256,256]{2,1,0:T(8,128)S(1)}, u32[]{:S(2)}) copy-start(s32[1,256,256]{2,1,0:T(8,128)S(1)} %and_or_fusion.refs_0_) | copy-start | bytes 786436
  1.1 50.0 %collective-permute-start = (s32[1,256,256]{2,1,0:T(8,128)S(1)}, s32[1,256,256]{2,1,0:T(8,128)S(1)}, u32[]{:S(2)}, u32[]{:S(2)}) collective-permute-start(s32[1,256,256]{2,1,0:T(8,128)S(1)} %and_or_fusion.refs_0_), channel_id=1, source_target_pairs={{0,128},{64,192},{128,256},{192,320},{256,384},{320,448},{384,0},{... | collective-permute-start | bytes 786440 | tf_op jit(solution)/shard_map/ppermute | solution.py:376
  5.1 49.5 %collective-permute-start.1 = (s32[1,256,256]{2,1,0:T(8,128)S(1)}, s32[1,256,256]{2,1,0:T(8,128)S(1)}, u32[]{:S(2)}, u32[]{:S(2)}) collective-permute-start(s32[1,256,256]{2,1,0:T(8,128)S(1)} %and_or_fusion.refs_0_), channel_id=1, source_target_pairs={{0,384},{64,448},{128,0},{192,64},{256,128},{320,192},{384,256},{4... | collective-permute-start | bytes 786440 | tf_op jit(solution)/shard_map/ppermute | solution.py:376
  8.3 48.2 %collective-permute-start.2 = (s32[1,256,256]{2,1,0:T(8,128)S(1)}, s32[1,256,256]{2,1,0:T(8,128)S(1)}, u32[]{:S(2)}, u32[]{:S(2)}) collective-permute-start(s32[1,256,256]{2,1,0:T(8,128)S(1)} %and_or_fusion.refs_0_), channel_id=1, source_target_pairs={{0,256},{64,320},{128,384},{192,448},{256,0},{320,64},{384,128},{4... | collective-permute-start | bytes 786440 | tf_op jit(solution)/shard_map/ppermute | solution.py:376
  11.9 60.3 %collective-permute-start.3 = (s32[1,256,256]{2,1,0:T(8,128)S(1)}, s32[1,256,256]{2,1,0:T(8,128)S(1)}, u32[]{:S(2)}, u32[]{:S(2)}) collective-permute-start(s32[1,256,256]{2,1,0:T(8,128)S(1)} %and_or_fusion.refs_0_), channel_id=1, source_target_pairs={{0,64},{64,0},{128,192},{192,128},{256,320},{320,256},{384,448},{4... | collective-permute-start | bytes 786440 | tf_op jit(solution)/shard_map/ppermute | solution.py:377
  20.4 23.6 %all-to-all-start = ((s32[64,1,1]{2,1,0:T(1,128)}), s32[64,1,1]{2,1,0:T(1,128)S(1)}, u32[]{:S(2)}, u32[]{:S(2)}) async-start(s32[64,1,1]{2,1,0:T(1,128)} %copy.12), calls=%async_computation | async-start | bytes 65536 | tf_op jit(solution)/shard_map/all_to_all | solution.py:346
  46.5 17.2 %all-to-all-start.1 = ((bf16[64,16,128]{2,1,0:T(8,128)(2,1)}), bf16[64,16,128]{2,1,0:T(8,128)(2,1)S(1)}, u32[]{:S(2)}, u32[]{:S(2)}) async-start(bf16[64,16,128]{2,1,0:T(8,128)(2,1)} %gather_fusion), calls=%async_computation.1 | async-start | bytes 524288 | tf_op jit(solution)/shard_map/all_to_all | solution.py:349
  51.2 21.1 %copy-start.5 = (s32[1,256,256]{2,1,0:T(8,128)}, s32[1,256,256]{2,1,0:T(8,128)S(1)}, u32[]{:S(2)}) copy-start(s32[1,256,256]{2,1,0:T(8,128)S(1)} %collective-permute-done.refs_1_) | copy-start | bytes 786436
  51.2 21.1 %collective-permute-start.4 = (s32[1,256,256]{2,1,0:T(8,128)S(1)}, s32[1,256,256]{2,1,0:T(8,128)S(1)}, u32[]{:S(2)}, u32[]{:S(2)}) collective-permute-start(s32[1,256,256]{2,1,0:T(8,128)S(1)} %collective-permute-done.refs_1_), channel_id=1, source_target_pairs={{0,64},{64,0},{128,192},{192,128},{256,320},{320,256},{384,448},{4... | collective-permute-start | bytes 786440 | tf_op jit(solution)/shard_map/ppermute | solution.py:378
  54.6 17.7 %copy-start.6 = (s32[1,256,256]{2,1,0:T(8,128)}, s32[1,256,256]{2,1,0:T(8,128)S(1)}, u32[]{:S(2)}) copy-start(s32[1,256,256]{2,1,0:T(8,128)S(1)} %collective-permute-done.1.refs_2_) | copy-start | bytes 786436
  54.6 17.7 %collective-permute-start.5 = (s32[1,256,256]{2,1,0:T(8,128)S(1)}, s32[1,256,256]{2,1,0:T(8,128)S(1)}, u32[]{:S(2)}, u32[]{:S(2)}) collective-permute-start(s32[1,256,256]{2,1,0:T(8,128)S(1)} %collective-permute-done.1.refs_2_), channel_id=1, source_target_pairs={{0,64},{64,0},{128,192},{192,128},{256,320},{320,256},{384,448},{4... | collective-permute-start | bytes 786440 | tf_op jit(solution)/shard_map/ppermute | solution.py:378
  56.5 15.8 %copy-start.7 = (s32[1,256,256]{2,1,0:T(8,128)}, s32[1,256,256]{2,1,0:T(8,128)S(1)}, u32[]{:S(2)}) copy-start(s32[1,256,256]{2,1,0:T(8,128)S(1)} %collective-permute-done.2.refs_3_) | copy-start | bytes 786436
  56.5 17.2 %collective-permute-start.6 = (s32[1,256,256]{2,1,0:T(8,128)S(1)}, s32[1,256,256]{2,1,0:T(8,128)}, u32[]{:S(2)}, u32[]{:S(2)}) collective-permute-start(s32[1,256,256]{2,1,0:T(8,128)S(1)} %collective-permute-done.2.refs_3_), channel_id=1, source_target_pairs={{0,64},{64,0},{128,192},{192,128},{256,320},{320,256},{384,448},{4... | collective-permute-start | bytes 786440 | tf_op jit(solution)/shard_map/ppermute | solution.py:378
  64.9 18.2 %all-to-all-start.2 = ((bf16[8,4,16,128]{3,2,1,0:T(8,128)(2,1)}), bf16[8,4,16,128]{3,2,1,0:T(8,128)(2,1)S(1)}, u32[]{:S(2)}, u32[]{:S(2)}) async-start(bf16[8,4,16,128]{3,2,1,0:T(8,128)(2,1)} %bitcast.5), calls=%async_computation.2 | async-start | bytes 262144 | tf_op jit(solution)/shard_map/all_to_all | solution.py:352
  72.2 0.7 copy-start.8
  72.3 0.8 copy-start.9
  73.1 0.7 copy-start.10
  83.2 0.7 copy-start.1
  95.4 4.8 %collective-permute-start.7 = (bf16[4,512,256]{2,1,0:T(8,128)(2,1)}, bf16[4,512,256]{2,1,0:T(8,128)(2,1)S(1)}, u32[]{:S(2)}, u32[]{:S(2)}) collective-permute-start(bf16[4,512,256]{2,1,0:T(8,128)(2,1)} %get-tuple-element.14), channel_id=1, source_target_pairs={{0,64},{64,0},{128,192},{192,128},{256,320},{320,256},{384,448},{4... | collective-permute-start | bytes 3145736 | tf_op jit(solution)/shard_map/ppermute | solution.py:385

commit v3 on v2

v3 whole, which is shorter than its diff:
```python
import functools
import math

import jax
import jax.numpy as jnp
import ml_dtypes
import numpy as np
from jax import lax
from jax.experimental import pallas as pl
from jax.experimental.pallas import tpu as pltpu
from jax.sharding import PartitionSpec as P


fresnel_strength = 9.0
softening = 0.01

CODE_TOP = 32766.0
REAL_MID = 1.0
REAL_HALF = 0.4
IMAG_HALF = 1.5


def tables(extent):
    indices = np.arange(extent)
    angles = (indices[:, None] * indices[None, :] % extent) * (2.0 * math.pi / extent)
    whole = np.cos(angles) + 1j * np.sin(angles)
    frequency = np.where(indices < (extent + 1) // 2, indices, indices - extent) / extent
    prop = (whole * np.exp(-1j * fresnel_strength * frequency**2)[None, :]) @ whole.conj() / extent
    four = whole.conj() / math.sqrt(extent)
    blocks = []
    for matrix in (prop, four):
        real = matrix.real.astype(np.float32).astype(ml_dtypes.bfloat16)
        imag = matrix.imag.astype(np.float32).astype(ml_dtypes.bfloat16)
        blocks.append(np.block([[real, -imag], [imag, real]]))
        blocks.append(np.block([[real, imag], [-imag, real]]))
    return np.stack(blocks).astype(ml_dtypes.bfloat16)


def encode(trans_real, trans_imag):
    real = jnp.round((trans_real - REAL_MID) * (CODE_TOP / REAL_HALF)).astype(jnp.int32)
    imag = jnp.round(trans_imag * (CODE_TOP / IMAG_HALF)).astype(jnp.int32)
    return (real << 16) | (imag & 0xFFFF)


def decode(code):
    real = (code >> 16).astype(jnp.float32) * (REAL_HALF / CODE_TOP) + REAL_MID
    imag = ((code << 16) >> 16).astype(jnp.float32) * (IMAG_HALF / CODE_TOP)
    return real, imag


def quarters(square):
    half = square.shape[0] // 2
    return (square[:half, :half], square[:half, half:], square[half:, :half], square[half:, half:])


def joined(a, b, c, d):
    return jnp.concatenate(
        [jnp.concatenate([a, b], axis=1), jnp.concatenate([c, d], axis=1)], axis=0
    )


def both_sides(left, right, field):
    real0, imag0, real1, imag1 = quarters(field)
    mid = jnp.dot(
        left, joined(real0, real1, imag0, imag1), preferred_element_type=jnp.float32
    ).astype(jnp.bfloat16)
    real0, real1, imag0, imag1 = quarters(mid)
    return jnp.dot(
        joined(real0, imag0, real1, imag1), right, preferred_element_type=jnp.float32
    )


def placed(offset_ref, position, side, tall):
    mine = lax.axis_index("cuts") * (offset_ref.shape[1] // lax.axis_size("cuts")) + position
    row_at = offset_ref[0, mine]
    start = jnp.minimum(row_at // 8, (side - tall) // 8) * 8
    return offset_ref[1, mine], pl.multiple_of(start, 8), row_at - start


def part(extent, pair, item):
    return pair * 2 + item, slice(item * extent, (item + 1) * extent)


def ask_kernel(index_ref, request_ref, *, stored):
    request_ref[...] = jnp.zeros_like(request_ref)
    for position in range(index_ref.shape[0]):
        index = index_ref[position]
        slot = jnp.full(request_ref.shape[1:], lax.rem(index, stored), request_ref.dtype)
        request_ref[lax.div(index, stored)] = slot


def pick_kernel(wanted_ref, shares_ref, rows_ref):
    for tile in range(rows_ref.shape[0]):
        rows_ref[tile] = shares_ref[wanted_ref[tile, 0, 0]]


def sort_kernel(index_ref, answered_ref, rows_ref, *, stored):
    for position in range(rows_ref.shape[0]):
        rows_ref[position] = answered_ref[lax.div(index_ref[position], stored)]


def descend_kernel(
    offset_ref,
    mine_hbm,
    theirs_hbm,
    table_hbm,
    probe_real_ref,
    probe_imag_ref,
    codes_hbm,
    wave_ref,
    table_ref,
    patch_ref,
    code_ref,
    table_sem,
    patch_sem,
    code_sem,
    *,
    steps,
):
    slices, count, extent, _ = code_ref.shape
    side = patch_ref.shape[-1]
    pairs = count // 2
    tall = extent + 8
    chips = len(steps)
    section_no = lax.axis_index("cuts")
    chip, core = section_no // 2, section_no % 2

    table_in = pltpu.make_async_copy(table_hbm.at[pl.ds(0, 2)], table_ref, table_sem)
    table_in.start()
    for place, step in enumerate(steps):
        came = (chip + chips - step) % chips * 2
        for hbm, layer in ((mine_hbm, came + core), (theirs_hbm, came + 1 - core)):
            pltpu.make_async_copy(hbm.at[place], patch_ref.at[layer], patch_sem.at[layer]).start()
    for pair in range(pairs):
        for item in range(2):
            _, rows = part(extent, pair, item)
            wave_ref[0, pair, rows, :extent] = probe_real_ref[...]
            wave_ref[0, pair, rows, extent:] = probe_imag_ref[...]
    table_in.wait()

    def code_out(layer):
        return pltpu.make_async_copy(code_ref.at[layer], codes_hbm.at[layer], code_sem.at[layer])

    def descend(layer, carry):
        pltpu.make_async_copy(mine_hbm.at[0], patch_ref.at[layer], patch_sem.at[layer]).wait()
        for pair in range(pairs):
            fields = []
            for item in range(2):
                position, rows = part(extent, pair, item)
                col_at, row_at, down = placed(offset_ref, position, side, tall)
                back = lax.rem(side - col_at, side)
                code = pltpu.roll(patch_ref[layer, pl.ds(row_at, tall), :], back, 1)[:, :extent]
                code = pltpu.roll(code, lax.rem(tall - down, tall), 0)[:extent]
                code_ref[layer, position] = code
                t_real, t_imag = decode(code)
                wave = wave_ref[layer, pair, rows, :].astype(jnp.float32)
                w_real, w_imag = wave[:, :extent], wave[:, extent:]
                fields.append(
                    jnp.concatenate(
                        [t_real * w_real - t_imag * w_imag, t_real * w_imag + t_imag * w_real], axis=1
                    ).astype(jnp.bfloat16)
                )
            ahead = both_sides(table_ref[0], table_ref[1], jnp.concatenate(fields, axis=0))
            wave_ref[layer + 1, pair] = ahead.astype(jnp.bfloat16)
        code_out(layer).start()
        return carry

    lax.fori_loop(0, slices, descend, 0)
    for layer in range(slices):
        code_out(layer).wait()


def ascend_kernel(
    offset_ref,
    table_hbm,
    amp_ref,
    codes_hbm,
    wave_ref,
    own_ref,
    other_ref,
    table_ref,
    code_ref,
    grad_ref,
    sum_ref,
    table_sem,
    code_sem,
):
    slices, count, extent, _ = code_ref.shape
    side = own_ref.shape[-1]
    pairs = count // 2
    pieces = amp_ref.shape[0]
    tall = extent + 8
    core = lax.axis_index("cuts") % 2

    def table_in(which):
        return pltpu.make_async_copy(
            table_hbm.at[pl.ds(2 * which, 2)], table_ref.at[pl.ds(2 * which, 2)], table_sem.at[which]
        )

    def code_in(layer):
        return pltpu.make_async_copy(codes_hbm.at[layer], code_ref.at[layer], code_sem.at[layer])

    table_in(1).start()
    table_in(0).start()
    for layer in reversed(range(slices)):
        code_in(layer).start()

    table_in(1).wait()
    for pair in range(pairs):
        far = both_sides(table_ref[2], table_ref[3], wave_ref[slices, pair])
        residue = []
        for item in range(2):
            position, rows = part(extent, pair, item)
            f_real, f_imag = far[rows, :extent], far[rows, extent:]
            amplitude = jnp.concatenate(
                [amp_ref[piece, position] for piece in range(pieces)], axis=0
            ).astype(jnp.float32)
            amp = jnp.sqrt(f_real * f_real + f_imag * f_imag + softening)
            ratio = (amp - amplitude) / amp
            residue.append(
                jnp.concatenate([ratio * f_real, ratio * f_imag], axis=1).astype(jnp.bfloat16)
            )
        back = both_sides(table_ref[3], table_ref[2], jnp.concatenate(residue, axis=0))
        grad_ref[pair] = back.astype(jnp.bfloat16)
    table_in(0).wait()

    def ascend(step, carry):
        layer = slices - 1 - step
        code_in(layer).wait()
        sum_ref[...] = jnp.zeros_like(sum_ref)
        for pair in range(pairs):
            back = both_sides(table_ref[1], table_ref[0], grad_ref[pair])
            for item in range(2):
                position, rows = part(extent, pair, item)
                u_real, u_imag = back[rows, :extent], back[rows, extent:]
                t_real, t_imag = decode(code_ref[layer, position])
                grad_ref[pair, rows, :extent] = (u_real * t_real + u_imag * t_imag).astype(jnp.bfloat16)
                grad_ref[pair, rows, extent:] = (u_imag * t_real - u_real * t_imag).astype(jnp.bfloat16)
                wave = wave_ref[layer, pair, rows, :].astype(jnp.float32)
                w_real, w_imag = wave[:, :extent], wave[:, extent:]
                col_at, row_at, down = placed(offset_ref, position, side, tall)
                for plane, contrib in enumerate(
                    (u_real * w_real + u_imag * w_imag, u_imag * w_real - u_real * w_imag)
                ):
                    high = jnp.concatenate(
                        [contrib, jnp.zeros((tall - extent, extent), jnp.float32)], axis=0
                    )
                    wide = jnp.concatenate(
                        [pltpu.roll(high, down, 0), jnp.zeros((tall, side - extent), jnp.float32)],
                        axis=1,
                    )
                    sum_ref[plane, pl.ds(row_at, tall), :] += pltpu.roll(wide, col_at, 1)
        mine = layer % 2 == core

        @pl.when(mine)
        def _():
            own_ref[layer // 2, :side] = sum_ref[0].astype(jnp.bfloat16)
            own_ref[layer // 2, side:] = sum_ref[1].astype(jnp.bfloat16)

        @pl.when(jnp.logical_not(mine))
        def _():
            other_ref[layer // 2, :side] = sum_ref[0].astype(jnp.bfloat16)
            other_ref[layer // 2, side:] = sum_ref[1].astype(jnp.bfloat16)

        return carry

    lax.fori_loop(0, slices, ascend, 0)


def in_hbm(array):
    return pltpu.with_memory_space_constraint(array, pltpu.HBM)


SMEM = pl.BlockSpec(memory_space=pltpu.SMEM)
VMEM = pl.BlockSpec(memory_space=pltpu.VMEM)
HBM = pl.BlockSpec(memory_space=pltpu.HBM)
FULL = 67_043_328


def leaving(room):
    return pltpu.CompilerParams(vmem_limit_bytes=FULL - room)


def small_call(kernel, shape, dtype, specs):
    return pl.pallas_call(
        kernel,
        out_shape=jax.ShapeDtypeStruct(shape, dtype),
        in_specs=specs,
        out_specs=VMEM,
        compiler_params=leaving(40 << 20),
    )


def forward(offsets, mine, theirs, probe_real, probe_imag, table, steps):
    chips, side, _ = mine.shape
    slices = 2 * chips
    extent = probe_real.shape[-1]
    count = offsets.shape[1] // lax.axis_size("cuts")
    square = (count // 2, 2 * extent, 2 * extent)
    return pl.pallas_call(
        functools.partial(descend_kernel, steps=steps),
        out_shape=(
            pltpu.HBM((slices, count, extent, extent), jnp.int32),
            jax.ShapeDtypeStruct((slices + 1,) + square, jnp.bfloat16),
        ),
        in_specs=[SMEM, HBM, HBM, HBM, VMEM, VMEM],
        out_specs=(HBM, VMEM),
        scratch_shapes=[
            pltpu.VMEM((2,) + table.shape[1:], table.dtype),
            pltpu.VMEM((slices, side, side), jnp.int32),
            pltpu.VMEM((slices, count, extent, extent), jnp.int32),
            pltpu.SemaphoreType.DMA,
            pltpu.SemaphoreType.DMA((slices,)),
            pltpu.SemaphoreType.DMA((slices,)),
        ],
        name="descend",
        compiler_params=leaving(40 << 20),
        cost_estimate=pl.CostEstimate(
            flops=2 * (slices + 1) * count * 8 * extent**3, bytes_accessed=6 << 20, transcendentals=0
        ),
    )(offsets, in_hbm(mine), in_hbm(theirs), in_hbm(table), probe_real, probe_imag)


def backward(offsets, table, amp_pieces, codes, waves, side):
    slices, count, extent, _ = codes.shape
    half = jax.ShapeDtypeStruct((slices // 2, 2 * side, side), jnp.bfloat16)
    square = (count // 2, 2 * extent, 2 * extent)
    return pl.pallas_call(
        ascend_kernel,
        out_shape=(half, half),
        in_specs=[SMEM, HBM, VMEM, HBM, VMEM],
        out_specs=(VMEM, VMEM),
        scratch_shapes=[
            pltpu.VMEM(table.shape, table.dtype),
            pltpu.VMEM((slices, count, extent, extent), jnp.int32),
            pltpu.VMEM(square, jnp.bfloat16),
            pltpu.VMEM((2, side, side), jnp.float32),
            pltpu.SemaphoreType.DMA((2,)),
            pltpu.SemaphoreType.DMA((slices,)),
        ],
        name="ascend",
        compiler_params=leaving(40 << 20),
        cost_estimate=pl.CostEstimate(
            flops=2 * (slices + 1) * count * 8 * extent**3, bytes_accessed=6 << 20, transcendentals=0
        ),
    )(offsets, in_hbm(table), amp_pieces, in_hbm(codes), waves)


def fetch_patterns(pattern_index, measured, sections):
    positions, extent, _ = measured.shape
    tile_count = lax.axis_size("tile")
    share = extent // sections
    ask = functools.partial(ask_kernel, stored=positions)
    request = small_call(ask, (tile_count, 1, 128), jnp.int32, [SMEM])(pattern_index)
    requested = lax.all_to_all(request, "tile", split_axis=0, concat_axis=0, tiled=True)
    first = lax.axis_index("cuts") * share
    shares = lax.dynamic_slice_in_dim(measured, first, share, 1)
    block = (share, extent)
    rows = small_call(pick_kernel, (tile_count,) + block, measured.dtype, [SMEM, VMEM])(
        requested, shares
    )
    answered = lax.all_to_all(rows, "tile", split_axis=0, concat_axis=0, tiled=True)
    sort = functools.partial(sort_kernel, stored=positions)
    pieces = small_call(sort, (positions,) + block, measured.dtype, [SMEM, VMEM])(
        pattern_index, answered
    )
    pieces = pieces.reshape(sections, positions // sections, share, extent)
    return lax.all_to_all(pieces, "cuts", split_axis=0, concat_axis=0, tiled=True)


def across(chips, step):
    return [(2 * at + core, 2 * ((at + step) % chips) + core) for at in range(chips) for core in range(2)]


def local(trans_real, trans_imag, probe_real, probe_imag, offsets, pattern_index, measured):
    extent = probe_real.shape[-1]
    side = trans_real.shape[-1]
    sections = lax.axis_size("cuts")
    chips = sections // 2
    sibling = [(at, at ^ 1) for at in range(sections)]
    steps = [0] + sorted(range(1, chips), key=lambda step: min(step, chips - step))

    table = jnp.asarray(tables(extent))
    amp_pieces = fetch_patterns(pattern_index, measured, sections)
    code = encode(trans_real, trans_imag)
    mine = [code]
    for step in steps[1:]:
        mine.append(lax.ppermute(code, "cuts", across(chips, step)))
    mine = jnp.concatenate(mine, axis=0)
    theirs = lax.ppermute(mine, "cuts", sibling)
    codes, waves = forward(offsets, mine, theirs, probe_real, probe_imag, table, steps)
    own, other = backward(offsets, table, amp_pieces, codes, waves, side)
    met = lax.ppermute(other, "cuts", sibling)
    paired = (own.astype(jnp.float32) + met.astype(jnp.float32)).astype(jnp.bfloat16)
    groups = [[2 * at + parity for at in range(chips)] for parity in range(2)]
    parts = lax.all_to_all(
        paired, "cuts", split_axis=0, concat_axis=0, tiled=True, axis_index_groups=groups
    )
    total = jnp.sum(parts.astype(jnp.float32), axis=0)
    return total.reshape(2, 1, side, side)


def solution(mesh):
    return jax.shard_map(
        local,
        mesh=mesh,
        in_specs=(
            P("cuts", "tile", None),
            P("cuts", "tile", None),
            P(),
            P(),
            P(None, "tile"),
            P("tile"),
            P("tile", None, None),
        ),
        out_specs=P(None, "cuts", "tile", None),
        check_vma=False,
    )
```

time: 122 us -> 121 us (level)
  blocking collectives: 18.3 us -> 35.1 us
  starting transfers between devices: 51.5 us -> 37.4 us
  waiting for transfers between devices: 15.4 us -> 22.9 us
  local copies, waits for them, and re-layouts: 6.99 us -> 1.55 us
  other arithmetic: 7.49 us -> 2.49 us
    all_to_all x0 -> x1, blocking collectives: none -> 16.3 us  [fetch_patterns(): lax.all_to_all(rows, 'tile', split_axis=0, concat_axis=0, tiled=True)]
    ppermute x7 -> x4, starting transfers between devices: 25.4 us -> 14.9 us  [the longest x3 10.8 us: local(): mine.append(lax.ppermute(code, 'cuts', across(chips, step)))]
    ppermute x7 -> x4, waiting for transfers between devices: 0.02 us -> 9.57 us  [the longest x3 9.56 us: local(): mine.append(lax.ppermute(code, 'cuts', across(chips, step)))]
    all_to_all x1 -> x0, starting transfers between devices: 4.62 us -> none  [fetch_patterns(): lax.all_to_all(rows, 'tile', split_axis=0, concat_axis=0, tiled=True)]
    all_to_all x1 -> x0, waiting for transfers between devices: 3.43 us -> none  [fetch_patterns(): lax.all_to_all(rows, 'tile', split_axis=0, concat_axis=0, tiled=True)]
    gather x2 -> x0, local copies, waits for them, and re-layouts: 2.56 us -> none  [the longest x1 1.32 us: fetch_patterns(): rows = mine.at[requested].get(mode='promise_in_bounds')]
    all_to_all x1, waiting for transfers between devices: 9.19 us -> 10.8 us  [fetch_patterns(): lax.all_to_all(request, 'tile', split_axis=0, concat_axis=0, tiled=True)]
    dynamic_slice x2 -> x1, local copies, waits for them, and re-layouts: 1.57 us -> 0.02 us  [fetch_patterns(): shares = lax.dynamic_slice_in_dim(measured, first, share, 1)]
  transfers between devices with their start and end apart: 11 -> 7, of which waited for: 3 -> 4; matrix products, arithmetic and copies ran while one was open for 7% -> 0% of each run, Pallas kernels for 8% -> 9%
where the time goes in v3:
time: 121 us
  starting transfers between devices  37.4 us (31%)
  blocking collectives  35.1 us (29%)
  waiting for transfers between devices  22.9 us (19%)
  Pallas kernels  21.1 us (17%)
  other arithmetic  2.49 us (2%)
  local copies, waits for them, and re-layouts  1.55 us (1%)
    all_to_all x1, blocking collectives, local(): lax.all_to_all(paired, 'cuts', split_axis=0, concat_axis=0, tiled=True, a...  18.7 us
    all_to_all x1, blocking collectives, fetch_patterns(): lax.all_to_all(rows, 'tile', split_axis=0, concat_axis=0, tiled=True)  16.3 us
    all_to_all x1, starting transfers between devices, fetch_patterns(): lax.all_to_all(request, 'tile', split_axis=0, concat_axis=0, tiled=True)  13.8 us
    ppermute x3, starting transfers between devices, local(): mine.append(lax.ppermute(code, 'cuts', across(chips, step)))  10.8 us
    all_to_all x1, waiting for transfers between devices, fetch_patterns(): lax.all_to_all(request, 'tile', split_axis=0, concat_axis=0, tiled=True)  10.8 us
    pallas_call x1, Pallas kernels, backward(): pl.pallas_call(ascend_kernel, out_shape=(half, half), in_specs=[SMEM, HBM...  9.68 us
    ppermute x3, waiting for transfers between devices, local(): mine.append(lax.ppermute(code, 'cuts', across(chips, step)))  9.56 us
    pallas_call x1, Pallas kernels, forward(): pl.pallas_call(functools.partial(descend_kernel, steps=steps), out_shape=...  7.79 us
  transfers between devices with their start and end apart: 7, of which 4 were waited for; matrix products, arithmetic and copies ran while one was open for 0% of the time, Pallas kernels for 9%

profile of v3, /device:TPU:1, one launch (start us, length us, event | category | flops | bytes accessed | tf_op | source)
XLA Modules:
  0.0 120.7 jit_solution(5243509377216349342)
XLA Ops:
  0.0 0.0 copy-start
  0.0 0.0 copy-start.1
  0.0 1.2 and_or_fusion
  1.2 0.0 copy-start.2
  1.2 5.5 %collective-permute-start.2 = (s32[1,256,256]{2,1,0:T(8,128)S(1)}, s32[1,256,256]{2,1,0:T(8,128)S(1)}, u32[]{:S(2)}, u32[]{:S(2)}) collective-permute-start(s32[1,256,256]{2,1,0:T(8,128)S(1)} %and_or_fusion), channel_id=1, source_target_pairs={{0,256},{64,320},{128,384},{192,448},{256,0},{320,64},{384,128},{4... | collective-permute-start | bytes 786440 | tf_op jit(solution)/shard_map/ppermute | solution.py:388
  6.7 2.8 %collective-permute-start.1 = (s32[1,256,256]{2,1,0:T(8,128)S(1)}, s32[1,256,256]{2,1,0:T(8,128)S(1)}, u32[]{:S(2)}, u32[]{:S(2)}) collective-permute-start(s32[1,256,256]{2,1,0:T(8,128)S(1)} %and_or_fusion), channel_id=1, source_target_pairs={{0,384},{64,448},{128,0},{192,64},{256,128},{320,192},{384,256},{4... | collective-permute-start | bytes 786440 | tf_op jit(solution)/shard_map/ppermute | solution.py:388
  9.5 2.5 %collective-permute-start = (s32[1,256,256]{2,1,0:T(8,128)S(1)}, s32[1,256,256]{2,1,0:T(8,128)S(1)}, u32[]{:S(2)}, u32[]{:S(2)}) collective-permute-start(s32[1,256,256]{2,1,0:T(8,128)S(1)} %and_or_fusion), channel_id=1, source_target_pairs={{0,128},{64,192},{128,256},{192,320},{256,384},{320,448},{384,0},{... | collective-permute-start | bytes 786440 | tf_op jit(solution)/shard_map/ppermute | solution.py:388
  12.0 0.0 collective-permute-done.2
  12.0 6.3 %collective-permute-done.1 = s32[1,256,256]{2,1,0:T(8,128)S(1)} collective-permute-done((s32[1,256,256]{2,1,0:T(8,128)S(1)}, s32[1,256,256]{2,1,0:T(8,128)S(1)}, u32[]{:S(2)}, u32[]{:S(2)}) %collective-permute-start.1) | collective-permute-done | bytes 262176 | tf_op jit(solution)/shard_map/ppermute | solution.py:388
  18.3 3.3 %collective-permute-done = s32[1,256,256]{2,1,0:T(8,128)S(1)} collective-permute-done((s32[1,256,256]{2,1,0:T(8,128)S(1)}, s32[1,256,256]{2,1,0:T(8,128)S(1)}, u32[]{:S(2)}, u32[]{:S(2)}) %collective-permute-start) | collective-permute-done | bytes 262176 | tf_op jit(solution)/shard_map/ppermute | solution.py:388
  21.6 0.1 pad_add_fusion.mine_hbm
  21.7 0.0 copy-start.5
  21.7 4.1 %collective-permute-start.3 = (s32[4,256,256]{2,1,0:T(8,128)S(1)}, s32[4,256,256]{2,1,0:T(8,128)}, u32[]{:S(2)}, u32[]{:S(2)}) collective-permute-start(s32[4,256,256]{2,1,0:T(8,128)S(1)} %pad_add_fusion.mine_hbm), channel_id=1, source_target_pairs={{0,64},{64,0},{128,192},{192,128},{256,320},{320,256},{384,448},{4... | collective-permute-start | bytes 3145736 | tf_op jit(solution)/shard_map/ppermute | solution.py:390
  25.8 0.0 copy-done.1
  25.8 1.2 %shard_map.82 = s32[64,1,128]{2,1,0:T(1,128)} custom-call(s32[32]{0:T(128)S(1)} %copy-done.1), custom_call_target="tpu_custom_call" | custom-call | tf_op jit(solution)/shard_map/pallas_call | solution.py:354
  27.1 13.8 %all-to-all-start = ((s32[64,1,128]{2,1,0:T(1,128)}), s32[64,1,128]{2,1,0:T(1,128)S(1)}, u32[]{:S(2)}, u32[]{:S(2)}) async-start(s32[64,1,128]{2,1,0:T(1,128)} %shard_map.82), calls=%async_computation | async-start | bytes 65536 | tf_op jit(solution)/shard_map/all_to_all | solution.py:355
  40.9 0.0 copy-done
  40.9 10.8 %all-to-all-done.wanted_ref = s32[64,1,128]{2,1,0:T(1,128)S(1)} async-done(((s32[64,1,128]{2,1,0:T(1,128)}), s32[64,1,128]{2,1,0:T(1,128)S(1)}, u32[]{:S(2)}, u32[]{:S(2)}) %all-to-all-start) | async-done | bytes 32800 | tf_op jit(solution)/shard_map/all_to_all | solution.py:355
  51.7 1.1 shard_map.83
  52.8 16.3 %all_to_all.20.answered_ref = bf16[64,16,128]{2,1,0:T(8,128)(2,1)S(1)} all-to-all(bf16[64,16,128]{2,1,0:T(8,128)(2,1)S(1)} %shard_map.83), channel_id=1, replica_groups=mesh['cuts'=8,'tile'=64] {'tile'}, dimensions={0} | all-to-all | bytes 524288 | tf_op jit(solution)/shard_map/all_to_all | solution.py:362
  69.2 1.3 %shard_map.84 = bf16[32,16,128]{2,1,0:T(8,128)(2,1)} custom-call(s32[32]{0:T(128)S(1)} %copy-done.1, bf16[64,16,128]{2,1,0:T(8,128)(2,1)S(1)} %all_to_all.20.answered_ref), custom_call_target="tpu_custom_call" | custom-call | tf_op jit(solution)/shard_map/pallas_call | solution.py:364
  70.4 6.7 %all-to-all-start.2 = ((bf16[8,4,16,128]{3,2,1,0:T(8,128)(2,1)}), bf16[8,4,16,128]{3,2,1,0:T(8,128)(2,1)S(1)}, u32[]{:S(2)}, u32[]{:S(2)}) async-start(bf16[8,4,16,128]{3,2,1,0:T(8,128)(2,1)} %bitcast), calls=%async_computation.2 | async-start | bytes 262144 | tf_op jit(solution)/shard_map/all_to_all | solution.py:368
  77.2 0.0 copy-done.5
  77.2 0.0 collective-permute-done.3.theirs_hbm
  77.2 0.0 copy-done.2
  77.2 0.0 copy-start.3
  77.2 0.7 copy-done.3
  77.9 0.0 copy-start.4
  77.9 0.8 copy-done.4
  78.7 7.8 %descend.1 = (s32[8,4,128,128]{3,2,1,0:T(8,128)}, bf16[9,2,256,256]{3,2,1,0:T(8,128)(2,1)S(1)}) custom-call(s32[2,32]{1,0:T(2,128)S(1)} %copy-done.2, s32[4,256,256]{2,1,0:T(8,128)} %copy-done.5, s32[4,256,256]{2,1,0:T(8,128)} %collective-permute-done.3.theirs_hbm, bf16[4,256,256]{2,1,0:T(8,128)(2,1)} %constant.26.clone.table_hbm, ...), custom_call_target="tpu_custom_call" | custom-call | flops 1207959552 | bytes 6291456 | tf_op jit(solution)/shard_map/descend/pallas_call | solution.py:300
  86.5 0.0 all-to-all-done.2.amp_ref
  86.5 9.7 %ascend.1 = (bf16[4,512,256]{2,1,0:T(8,128)(2,1)S(1)}, bf16[4,512,256]{2,1,0:T(8,128)(2,1)S(1)}) custom-call(s32[2,32]{1,0:T(2,128)S(1)} %copy-done.2, bf16[4,256,256]{2,1,0:T(8,128)(2,1)} %constant.26.clone.table_hbm, bf16[8,4,16,128]{3,2,1,0:T(8,128)(2,1)S(1)} %all-to-all-done.2.amp_ref, s32[8,4,128,128]{3,2,1,0:T(8,128)} %get-tuple-element.9.codes_hbm, ...), custom_call_target="tpu_custom_call" | custom-call | flops 1207959552 | bytes 6291456 | tf_op jit(solution)/shard_map/ascend/pallas_call | solution.py:328
  96.2 1.9 %collective-permute-start.4 = (bf16[4,512,256]{2,1,0:T(8,128)(2,1)S(1)}, bf16[4,512,256]{2,1,0:T(8,128)(2,1)S(1)}, u32[]{:S(2)}, u32[]{:S(2)}) collective-permute-start(bf16[4,512,256]{2,1,0:T(8,128)(2,1)S(1)} %get-tuple-element.12), channel_id=1, source_target_pairs={{0,64},{64,0},{128,192},{192,128},{256,320},{320,256},{384,448},{4... | collective-permute-start | bytes 3145736 | tf_op jit(solution)/shard_map/ppermute | solution.py:393
  98.1 2.6 %collective-permute-done.4 = bf16[4,512,256]{2,1,0:T(8,128)(2,1)S(1)} collective-permute-done((bf16[4,512,256]{2,1,0:T(8,128)(2,1)S(1)}, bf16[4,512,256]{2,1,0:T(8,128)(2,1)S(1)}, u32[]{:S(2)}, u32[]{:S(2)}) %collective-permute-start.4) | collective-permute-done | bytes 1048608 | tf_op jit(solution)/shard_map/ppermute | solution.py:393
  100.7 0.3 add_convert_fusion
  101.0 18.7 %all_to_all.21 = bf16[4,512,256]{2,1,0:T(8,128)(2,1)S(1)} all-to-all(bf16[4,512,256]{2,1,0:T(8,128)(2,1)S(1)} %add_convert_fusion), channel_id=1, replica_groups={{0,128,256,384},{64,192,320,448},{1,129,257,385},{65,193,321,449},{2,13..., dimensions={0} | all-to-all | bytes 2097152 | tf_op jit(solution)/shard_map/all_to_all | solution.py:396
  119.8 0.9 convert_reduce_fusion
  (1 shorter events, 0.0 us)
Async XLA Ops:
  0.0 40.9 %copy-start = (bf16[32,128,128]{2,1,0:T(8,128)(2,1)S(1)}, bf16[32,128,128]{2,1,0:T(8,128)(2,1)}, u32[]{:S(2)}) copy-start(bf16[32,128,128]{2,1,0:T(8,128)(2,1)} %param.14) | copy-start | bytes 3145732
  0.0 25.8 %copy-start.1 = (s32[32]{0:T(128)S(1)}, s32[32]{0:T(128)}, u32[]{:S(2)}) copy-start(s32[32]{0:T(128)} %index_ref.3) | copy-start | bytes 388
  1.2 76.0 %copy-start.2 = (s32[2,32]{1,0:T(2,128)S(1)}, s32[2,32]{1,0:T(2,128)}, u32[]{:S(2)}) copy-start(s32[2,32]{1,0:T(2,128)} %offset_ref.3) | copy-start | bytes 772
  1.2 10.8 %collective-permute-start.2 = (s32[1,256,256]{2,1,0:T(8,128)S(1)}, s32[1,256,256]{2,1,0:T(8,128)S(1)}, u32[]{:S(2)}, u32[]{:S(2)}) collective-permute-start(s32[1,256,256]{2,1,0:T(8,128)S(1)} %and_or_fusion), channel_id=1, source_target_pairs={{0,256},{64,320},{128,384},{192,448},{256,0},{320,64},{384,128},{4... | collective-permute-start | bytes 786440 | tf_op jit(solution)/shard_map/ppermute | solution.py:388
  6.7 11.6 %collective-permute-start.1 = (s32[1,256,256]{2,1,0:T(8,128)S(1)}, s32[1,256,256]{2,1,0:T(8,128)S(1)}, u32[]{:S(2)}, u32[]{:S(2)}) collective-permute-start(s32[1,256,256]{2,1,0:T(8,128)S(1)} %and_or_fusion), channel_id=1, source_target_pairs={{0,384},{64,448},{128,0},{192,64},{256,128},{320,192},{384,256},{4... | collective-permute-start | bytes 786440 | tf_op jit(solution)/shard_map/ppermute | solution.py:388
  9.5 12.1 %collective-permute-start = (s32[1,256,256]{2,1,0:T(8,128)S(1)}, s32[1,256,256]{2,1,0:T(8,128)S(1)}, u32[]{:S(2)}, u32[]{:S(2)}) collective-permute-start(s32[1,256,256]{2,1,0:T(8,128)S(1)} %and_or_fusion), channel_id=1, source_target_pairs={{0,128},{64,192},{128,256},{192,320},{256,384},{320,448},{384,0},{... | collective-permute-start | bytes 786440 | tf_op jit(solution)/shard_map/ppermute | solution.py:388
  21.7 55.5 %copy-start.5 = (s32[4,256,256]{2,1,0:T(8,128)}, s32[4,256,256]{2,1,0:T(8,128)S(1)}, u32[]{:S(2)}) copy-start(s32[4,256,256]{2,1,0:T(8,128)S(1)} %pad_add_fusion.mine_hbm) | copy-start | bytes 3145732
  21.7 55.5 %collective-permute-start.3 = (s32[4,256,256]{2,1,0:T(8,128)S(1)}, s32[4,256,256]{2,1,0:T(8,128)}, u32[]{:S(2)}, u32[]{:S(2)}) collective-permute-start(s32[4,256,256]{2,1,0:T(8,128)S(1)} %pad_add_fusion.mine_hbm), channel_id=1, source_target_pairs={{0,64},{64,0},{128,192},{192,128},{256,320},{320,256},{384,448},{4... | collective-permute-start | bytes 3145736 | tf_op jit(solution)/shard_map/ppermute | solution.py:390
  27.1 24.6 %all-to-all-start = ((s32[64,1,128]{2,1,0:T(1,128)}), s32[64,1,128]{2,1,0:T(1,128)S(1)}, u32[]{:S(2)}, u32[]{:S(2)}) async-start(s32[64,1,128]{2,1,0:T(1,128)} %shard_map.82), calls=%async_computation | async-start | bytes 65536 | tf_op jit(solution)/shard_map/all_to_all | solution.py:355
  70.4 16.1 %all-to-all-start.2 = ((bf16[8,4,16,128]{3,2,1,0:T(8,128)(2,1)}), bf16[8,4,16,128]{3,2,1,0:T(8,128)(2,1)S(1)}, u32[]{:S(2)}, u32[]{:S(2)}) async-start(bf16[8,4,16,128]{3,2,1,0:T(8,128)(2,1)} %bitcast), calls=%async_computation.2 | async-start | bytes 262144 | tf_op jit(solution)/shard_map/all_to_all | solution.py:368
  77.2 0.8 copy-start.3
  77.9 0.8 copy-start.4
  96.2 4.6 %collective-permute-start.4 = (bf16[4,512,256]{2,1,0:T(8,128)(2,1)S(1)}, bf16[4,512,256]{2,1,0:T(8,128)(2,1)S(1)}, u32[]{:S(2)}, u32[]{:S(2)}) collective-permute-start(bf16[4,512,256]{2,1,0:T(8,128)(2,1)S(1)} %get-tuple-element.12), channel_id=1, source_target_pairs={{0,64},{64,0},{128,192},{192,128},{256,320},{320,256},{384,448},{4... | collective-permute-start | bytes 3145736 | tf_op jit(solution)/shard_map/ppermute | solution.py:393
